TPU v7x, 128 devices: a whole 4x4x4 slice. The times are simulated.
128 devices in a mesh: grp: 4 (over z_hi, core), ep: 32 (over y, x, z_lo).
Axes of the slice: x: 4, y: 4, z: 4 (z_hi: 2, z_lo: 2; z = z_hi * 2 + z_lo), core: 2. Of those that a mesh axis runs over, the one named last changes fastest.
Arguments:
- hidden: bfloat16 [16384, 8, 768], P(('grp', 'ep')), may hold values from -1.5 to 1.5
- out_grad: bfloat16 [16384, 4096], P(('grp', 'ep')), may hold values from -6 to 6
- route_ids: int32 [16384, 8], P(('grp', 'ep')), may hold values from 0 to 127, all different within a row; in each aligned block of 128 rows (0 to 127, 128 to 255, ...) at most 12 rows name the same one
- gate_vals: float32 [16384, 8], P(('grp', 'ep')), may hold values from 0.05 to 0.5
- rollout_ids: int32 [128, 128], P(('grp', 'ep')), may hold values from 0 to 3, never falling along the last dimension, each value on 1 to 64 neighbouring positions
- advantages: float32 [128, 4], P(('grp', 'ep')), may hold values from -3 to 3
- down_weight: bfloat16 [128, 768, 4096], P(('grp', 'ep')), may hold values from -0.09375 to 0.09375
Outputs:
- hidden_grad: bfloat16 [16384, 8, 768], P(('grp', 'ep'))
- weight_grad: bfloat16 [128, 768, 4096], P(('grp', 'ep'))
Inputs may be any that keep to these rules, and one draw needn't show every extreme that they name: `route_ids`: each row names 8 different experts; among the 128 rows of one device no expert is named more than 12 times, a bound that some block reaches there. `rollout_ids`: within each row the ids never fall; every id 0 to 3 appears, at most 128 // 2 times.
All inputs are finite; a program needn't handle non-finite values.
Results may differ from a plain program's by a relative error of at most 0.0049.
Values may be sent and summed in bfloat16 or wider, within the bound.
A program may use at most 192 MiB of HBM per device.

v0:
```python
import jax
import jax.numpy as jnp
from jax import lax
from jax.sharding import PartitionSpec as P


def shards(hidden, out_grad, route_ids, gate_vals, rollout_ids, advantages, down_weight):
    tokens_dev = out_grad.shape[0]
    top_count = route_ids.shape[1]
    hidden_width = hidden.shape[2]
    model_width = out_grad.shape[1]
    rollouts = advantages.shape[1]
    group_count = lax.axis_size("grp")
    owner_count = lax.axis_size("ep")
    experts = group_count * owner_count
    capacity = max(2, tokens_dev * top_count * 3 // (2 * experts))
    slots_dev = tokens_dev * top_count
    member = (rollout_ids[0][:, None] == jnp.arange(rollouts, dtype=jnp.int32)[None, :]).astype(
        jnp.float32
    )
    counts = jnp.sum(member, axis=0)
    roll_weight = advantages[0] * (tokens_dev / rollouts) / counts
    token_weight = jnp.sum(member * roll_weight[None, :], axis=1)
    slot_scale = gate_vals * token_weight[:, None]
    scaled = (slot_scale[:, :, None] * out_grad[:, None, :].astype(jnp.float32)).astype(
        jnp.bfloat16
    )
    scaled = scaled.reshape(slots_dev, model_width)
    flat_ids = route_ids.reshape(slots_dev)
    one_hot = (flat_ids[:, None] == jnp.arange(experts, dtype=jnp.int32)[None, :]).astype(
        jnp.bfloat16
    )
    slot_index = jnp.arange(slots_dev, dtype=jnp.int32)
    earlier = (slot_index[:, None] > slot_index[None, :]).astype(jnp.bfloat16)
    before = jnp.dot(earlier, one_hot, preferred_element_type=jnp.float32)
    slot_rank = jnp.sum(before * one_hot.astype(jnp.float32), axis=1).astype(jnp.int32)
    position = flat_ids * capacity + slot_rank
    source = jnp.full((experts * capacity,), slots_dev, jnp.int32).at[position].set(slot_index)
    hidden_pad = jnp.concatenate(
        [hidden.reshape(slots_dev, hidden_width), jnp.zeros((1, hidden_width), jnp.bfloat16)],
        axis=0,
    )
    scaled_pad = jnp.concatenate([scaled, jnp.zeros((1, model_width), jnp.bfloat16)], axis=0)
    hidden_send = hidden_pad[source]
    scaled_send = scaled_pad[source]
    arrived = (
        lax.all_to_all(
            hidden_send.reshape(experts, capacity, hidden_width),
            ("grp", "ep"),
            split_axis=0,
            concat_axis=0,
            tiled=True,
        ),
        lax.all_to_all(
            scaled_send.reshape(experts, capacity, model_width),
            ("grp", "ep"),
            split_axis=0,
            concat_axis=0,
            tiled=True,
        ),
    )
    got_hidden = arrived[0].reshape(experts * capacity, hidden_width)
    got_scaled = arrived[1].reshape(experts * capacity, model_width)
    weight = down_weight[0]
    weight_grad = lax.dot_general(
        got_hidden, got_scaled, (((0,), (0,)), ((), ())), preferred_element_type=jnp.float32
    )
    answers = lax.dot_general(
        got_scaled, weight, (((1,), (1,)), ((), ())), preferred_element_type=jnp.float32
    ).astype(jnp.bfloat16)
    returned = lax.all_to_all(
        answers.reshape(experts, capacity, hidden_width),
        ("grp", "ep"),
        split_axis=0,
        concat_axis=0,
        tiled=True,
    )
    returned = returned.reshape(experts * capacity, hidden_width)
    hidden_grad = returned[position].reshape(tokens_dev, top_count, hidden_width)
    return (hidden_grad, weight_grad.astype(jnp.bfloat16)[None])


def solution(mesh):
    placed = (
        P(("grp", "ep"), None, None),
        P(("grp", "ep"), None),
        P(("grp", "ep"), None),
        P(("grp", "ep"), None),
        P(("grp", "ep"), None),
        P(("grp", "ep"), None),
        P(("grp", "ep"), None, None),
    )
    return jax.shard_map(
        shards,
        mesh=mesh,
        in_specs=placed,
        out_specs=(P(("grp", "ep"), None, None), P(("grp", "ep"), None, None)),
        check_vma=False,
    )
```

profile of v0, /device:TPU:1, one launch (start us, length us, event | category | flops | bytes accessed | tf_op | source)
XLA Modules:
  0.0 450.2 jit_solution(16657203044910072932)
XLA Ops:
  0.6 0.7 broadcast_multiply_fusion
  1.3 0.8 copy.22
  2.1 1.4 convert_element_type.38
  3.5 0.8 convert_reduce_fusion
  4.3 0.7 fusion.21
  5.0 0.7 select_reduce_fusion
  5.7 0.7 broadcast_multiply_fusion.1
  6.4 0.1 copy.20
  6.5 0.1 mul.65
  6.6 0.1 copy.21
  6.7 0.1 mul.72
  6.9 0.6 fusion.16
  7.6 4.3 scatter_custom_fusion
  11.9 5.4 %fusion = bf16[1024,4096]{1,0:T(8,128)(2,1)} fusion(f32[128,4096]{1,0:T(8,128)S(1)} %convert_element_type.38, f32[1024]{0:T(1024)S(1)} %mul.65), kind=kLoop, calls=%fused_computation.5 | loop fusion | flops 8388608 | bytes 10489856 | tf_op jit(solution)/shard_map/convert_element_type | solution.py:25
  17.3 7.7 %concatenate.6 = bf16[1025,4096]{1,0:T(8,128)(2,1)} pad(bf16[1024,4096]{1,0:T(8,128)(2,1)} %fusion, bf16[]{:T(256)} %constant.1.clone.1), padding=0_1x0_0 | pad | bytes 16785410 | tf_op jit(solution)/shard_map/concatenate | solution.py:43
  25.0 26.5 %gather_fusion = bf16[1536,4096]{1,0:T(8,128)(2,1)} fusion(bf16[1025,4096]{1,0:T(8,128)(2,1)} %concatenate.6, s32[2048]{0:T(1024)S(1)} %pad_clamp_fusion), kind=kCustom, calls=%fused_computation | custom fusion | bytes 25171968 | tf_op jit(solution)/shard_map/gather | solution.py:45
  51.5 17.9 %reshape.70 = bf16[128,12,4096]{2,1,0:T(8,128)(2,1)} reshape(bf16[1536,4096]{1,0:T(8,128)(2,1)} %gather_fusion) | data formatting | bytes 25165824 | tf_op jit(solution)/shard_map/reshape | solution.py:55
  69.4 12.0 %all-to-all-start = ((bf16[128,12,4096]{2,1,0:T(8,128)(2,1)}), bf16[128,12,4096]{2,1,0:T(8,128)(2,1)}, u32[]{:S(2)}, u32[]{:S(2)}) async-start(bf16[128,12,4096]{2,1,0:T(8,128)(2,1)} %reshape.70), calls=%async_computation | async-start | bytes 33554432 | tf_op jit(solution)/shard_map/all_to_all | solution.py:54
  81.4 0.1 concatenate.7
  81.5 5.6 %gather_fusion.2 = bf16[1536,768]{1,0:T(8,128)(2,1)} fusion(bf16[1025,768]{1,0:T(8,128)(2,1)S(1)} %concatenate.7, s32[2048]{0:T(1024)S(1)} %pad_clamp_fusion), kind=kCustom, calls=%fused_computation.2 | custom fusion | bytes 4724736 | tf_op jit(solution)/shard_map/gather | solution.py:44
  87.1 4.9 %reshape.76 = bf16[128,12,768]{2,1,0:T(8,128)(2,1)} reshape(bf16[1536,768]{1,0:T(8,128)(2,1)} %gather_fusion.2) | data formatting | bytes 4718592 | tf_op jit(solution)/shard_map/reshape | solution.py:48
  92.0 238.1 %all-to-all-done = bf16[128,12,4096]{2,1,0:T(8,128)(2,1)} async-done(((bf16[128,12,4096]{2,1,0:T(8,128)(2,1)}), bf16[128,12,4096]{2,1,0:T(8,128)(2,1)}, u32[]{:S(2)}, u32[]{:S(2)}) %all-to-all-start) | async-done | bytes 12582944 | tf_op jit(solution)/shard_map/all_to_all | solution.py:54
  330.1 20.8 %all-to-all-start.2 = ((bf16[128,12,768]{2,1,0:T(8,128)(2,1)}), bf16[128,12,768]{2,1,0:T(8,128)(2,1)S(1)}, u32[]{:S(2)}, u32[]{:S(2)}) async-start(bf16[128,12,768]{2,1,0:T(8,128)(2,1)} %reshape.76), calls=%async_computation.2 | async-start | bytes 6291456 | tf_op jit(solution)/shard_map/all_to_all | solution.py:47
  350.9 18.2 %reshape.71 = bf16[1536,4096]{1,0:T(8,128)(2,1)} reshape(bf16[128,12,4096]{2,1,0:T(8,128)(2,1)} %all-to-all-done) | data formatting | bytes 25165824 | tf_op jit(solution)/shard_map/reshape | solution.py:63
  369.1 15.8 %fusion.11 = bf16[1536,768]{1,0:T(8,128)(2,1)} fusion(bf16[1536,4096]{1,0:T(8,128)(2,1)} %reshape.71, bf16[1,768,4096]{2,1,0:T(8,128)(2,1)} %param.13), kind=kOutput, calls=%fused_computation.14 | convolution fusion | flops 9664856064 | bytes 21233664 | tf_op jit(solution)/shard_map/dot_general | solution.py:68
  384.9 4.9 %reshape.72 = bf16[128,12,768]{2,1,0:T(8,128)(2,1)} reshape(bf16[1536,768]{1,0:T(8,128)(2,1)} %fusion.11) | data formatting | bytes 4718592 | tf_op jit(solution)/shard_map/reshape | solution.py:72
  389.8 2.9 all-to-all-done.2
  392.6 7.3 %all-to-all-start.1 = ((bf16[128,12,768]{2,1,0:T(8,128)(2,1)}), bf16[128,12,768]{2,1,0:T(8,128)(2,1)}, u32[]{:S(2)}, u32[]{:S(2)}) async-start(bf16[128,12,768]{2,1,0:T(8,128)(2,1)} %reshape.72), calls=%async_computation.1 | async-start | bytes 6291456 | tf_op jit(solution)/shard_map/all_to_all | solution.py:71
  400.0 30.8 %fusion.7 = bf16[1,768,4096]{2,1,0:T(8,128)(2,1)} fusion(bf16[128,12,4096]{2,1,0:T(8,128)(2,1)} %all-to-all-done, bf16[128,12,768]{2,1,0:T(8,128)(2,1)S(1)} %all-to-all-done.2), kind=kOutput, calls=%fused_computation.11 | convolution fusion | flops 9666822144 | bytes 21233664 | tf_op jit(solution)/shard_map/dot_general | solution.py:65
  430.8 10.6 %all-to-all-done.1 = bf16[128,12,768]{2,1,0:T(8,128)(2,1)} async-done(((bf16[128,12,768]{2,1,0:T(8,128)(2,1)}), bf16[128,12,768]{2,1,0:T(8,128)(2,1)}, u32[]{:S(2)}, u32[]{:S(2)}) %all-to-all-start.1) | async-done | bytes 2359328 | tf_op jit(solution)/shard_map/all_to_all | solution.py:71
  441.4 3.6 reshape.73
  445.0 5.2 %gather_fusion.1 = bf16[1024,768]{1,0:T(8,128)(2,1)} fusion(bf16[1536,768]{1,0:T(8,128)(2,1)S(1)} %reshape.73, s32[1024]{0:T(1024)S(1)} %broadcast_clamp_fusion), kind=kCustom, calls=%fused_computation.1 | custom fusion | bytes 3149824 | tf_op jit(solution)/shard_map/gather | solution.py:79
  (9 shorter events, 0.1 us)
Async XLA Ops:
  69.4 12.0 %copy-start = (bf16[128,8,768]{2,1,0:T(8,128)(2,1)S(1)}, bf16[128,8,768]{2,1,0:T(8,128)(2,1)}, u32[]{:S(2)}) copy-start(bf16[128,8,768]{2,1,0:T(8,128)(2,1)} %param.7) | copy-start | bytes 4718596
  69.4 260.7 %all-to-all-start = ((bf16[128,12,4096]{2,1,0:T(8,128)(2,1)}), bf16[128,12,4096]{2,1,0:T(8,128)(2,1)}, u32[]{:S(2)}, u32[]{:S(2)}) async-start(bf16[128,12,4096]{2,1,0:T(8,128)(2,1)} %reshape.70), calls=%async_computation | async-start | bytes 33554432 | tf_op jit(solution)/shard_map/all_to_all | solution.py:54
  330.1 62.5 %all-to-all-start.2 = ((bf16[128,12,768]{2,1,0:T(8,128)(2,1)}), bf16[128,12,768]{2,1,0:T(8,128)(2,1)S(1)}, u32[]{:S(2)}, u32[]{:S(2)}) async-start(bf16[128,12,768]{2,1,0:T(8,128)(2,1)} %reshape.76), calls=%async_computation.2 | async-start | bytes 6291456 | tf_op jit(solution)/shard_map/all_to_all | solution.py:47
  392.6 48.7 %all-to-all-start.1 = ((bf16[128,12,768]{2,1,0:T(8,128)(2,1)}), bf16[128,12,768]{2,1,0:T(8,128)(2,1)}, u32[]{:S(2)}, u32[]{:S(2)}) async-start(bf16[128,12,768]{2,1,0:T(8,128)(2,1)} %reshape.72), calls=%async_computation.1 | async-start | bytes 6291456 | tf_op jit(solution)/shard_map/all_to_all | solution.py:71
where the time goes:
time: 452 us; the launch traced here: 450 us
  waiting for transfers between devices  252 us (56%)
  local copies, waits for them, and re-layouts  100 us (22%)
  matrix products  47.2 us (10%)
  starting transfers between devices  40.1 us (9%)
  other arithmetic  10.4 us (2%)
    all_to_all x1, waiting for transfers between devices, shards(): lax.all_to_all(scaled_send.reshape(experts, capacity, model_width), ('grp...  238 us
    dot_general x1, matrix products, shards(): lax.dot_general(got_hidden, got_scaled, (((0,), (0,)), ((), ())), preferr...  30.8 us
    gather x1, local copies, waits for them, and re-layouts, shards(): scaled_send = scaled_pad[source]  26.5 us
    all_to_all x1, starting transfers between devices, shards(): lax.all_to_all(hidden_send.reshape(experts, capacity, hidden_width), ('gr...  20.8 us
    reshape x1, local copies, waits for them, and re-layouts, shards(): got_scaled = arrived[1].reshape(experts * capacity, model_width)  18.2 us
    reshape x1, local copies, waits for them, and re-layouts, shards(): scaled_send.reshape(experts, capacity, model_width)  17.9 us
    dot_general x1, matrix products, shards(): lax.dot_general(got_scaled, weight, (((1,), (1,)), ((), ())), preferred_e...  15.8 us
    all_to_all x1, starting transfers between devices, shards(): lax.all_to_all(scaled_send.reshape(experts, capacity, model_width), ('grp...  12 us
  transfers between devices with their start and end apart: 3, of which 3 were waited for; matrix products, arithmetic and copies ran while one was open for 18% of the time, Pallas kernels for 0%

commit v1 on v0

v1 whole, which is shorter than its diff:
```python
import functools

import jax
import jax.numpy as jnp
from jax import lax
from jax.experimental import pallas as pl
from jax.experimental.pallas import tpu as pltpu
from jax.sharding import PartitionSpec as P

MESH = pl.DeviceIdType.MESH
SIDE = 4
CAP = 12
PICK = SIDE * CAP
WIDTHS = (1408, 1408, 1280)
STARTS = (0, 1408, 2816)


def position():
    group, owner = lax.axis_index("grp"), lax.axis_index("ep")
    core = group % 2
    z = (group // 2) * 2 + owner % 2
    x = (owner // 2) % 4
    y = owner // 8
    return (x, y, z), core


def place(coords, core):
    x, y, z = coords
    return ((z // 2) * 2 + core, y * 8 + x * 2 + z % 2)


def moved(coords, axis, by):
    new = list(coords)
    new[axis] = (coords[axis] + by) % SIDE
    return tuple(new)


def expert_rows(part):
    row = lax.broadcasted_iota(jnp.int32, (128, 128), 0)
    coords = [None] * 3
    coords[part % 3] = row // 32
    coords[(part + 1) % 3] = (row // 8) % 4
    coords[(part + 2) % 3] = (row // 2) % 4
    x, y, z = coords
    return ((z // 2) * 2 + row % 2) * 32 + y * 8 + x * 2 + z % 2


def dispatch_kernel(
    route_ref,
    gate_ref,
    rollout_ref,
    adv_ref,
    grad_ref,
    out0,
    out1,
    out2,
    lines0,
    lines1,
    lines2,
    tables,
    got_tables,
    picks,
    send0,
    send1,
    send2,
    mid0,
    mid1,
    mid2,
    local_sem,
    line_send,
    line_recv,
    table_send,
    table_recv,
    mid_send,
    mid_recv,
    last_send,
    last_recv,
):
    outs, lines = (out0, out1, out2), (lines0, lines1, lines2)
    sends, mids = (send0, send1, send2), (mid0, mid1, mid2)
    here, core = position()

    barrier = pltpu.get_barrier_semaphore()
    for axis in range(3):
        for by in range(SIDE):
            for flip in range(2):
                if (by or flip) and (by or axis == 0):
                    pl.semaphore_signal(
                        barrier,
                        inc=1,
                        device_id=place(moved(here, axis, by), (core + flip) % 2),
                        device_id_type=MESH,
                    )
    pl.semaphore_wait(barrier, 19)

    def line_copy(part, by):
        there = place(moved(here, part, by), core)
        return pltpu.make_async_remote_copy(
            src_ref=grad_ref.at[:, pl.ds(STARTS[part], WIDTHS[part])],
            dst_ref=lines[part].at[pl.ds(pl.multiple_of(here[part] * 128, 128), 128)],
            send_sem=line_send.at[part, by],
            recv_sem=line_recv.at[part, by],
            device_id=there,
            device_id_type=MESH,
        )

    def own_line(part):
        return pltpu.make_async_copy(
            grad_ref.at[:, pl.ds(STARTS[part], WIDTHS[part])],
            lines[part].at[pl.ds(pl.multiple_of(here[part] * 128, 128), 128)],
            local_sem.at[part],
        )

    def table_copy(part, by):
        target = moved(here, part, by)
        return pltpu.make_async_remote_copy(
            src_ref=tables.at[part, target[part]],
            dst_ref=got_tables.at[part, here[part]],
            send_sem=table_send.at[part, by],
            recv_sem=table_recv.at[part, by],
            device_id=place(target, core),
            device_id_type=MESH,
        )

    def own_table(part):
        return pltpu.make_async_copy(
            tables.at[part, here[part]], got_tables.at[part, here[part]], local_sem.at[3 + part]
        )

    for by in (1, 3, 2):
        for part in range(3):
            line_copy(part, by).start()
    for part in range(3):
        own_line(part).start()

    rollout = rollout_ref[...]
    weight = jnp.zeros((1, 128), jnp.float32)
    for i in range(4):
        hit = (rollout == i).astype(jnp.float32)
        count = jnp.sum(hit, axis=1, keepdims=True)
        weight = weight + hit * (adv_ref[:, i : i + 1] * 32.0 / count)
    scale = gate_ref[...] * weight
    route = route_ref[...]
    sooner = (
        lax.broadcasted_iota(jnp.int32, (128, 128), 0)
        < lax.broadcasted_iota(jnp.int32, (128, 128), 1)
    ).astype(jnp.bfloat16)
    for part in range(3):
        expert = expert_rows(part)
        named = jnp.zeros((128, 128), jnp.float32)
        held = jnp.zeros((128, 128), jnp.float32)
        for k in range(8):
            match = route[k : k + 1, :] == expert
            named = named + jnp.where(match, 1.0, 0.0)
            held = held + jnp.where(match, scale[k : k + 1, :], 0.0)
        rank = jnp.dot(named.astype(jnp.bfloat16), sooner, preferred_element_type=jnp.float32)
        rank = jnp.where(named > 0.5, rank, -1.0)
        for i in range(SIDE):
            tables[part, i, 0:32] = rank[32 * i : 32 * i + 32]
            tables[part, i, 32:64] = held[32 * i : 32 * i + 32]
    for by in (1, 3, 2):
        for part in range(3):
            table_copy(part, by).start()
    for part in range(3):
        own_table(part).start()

    def mid_copy(part, by):
        return pltpu.make_async_remote_copy(
            src_ref=sends[part].at[by],
            dst_ref=mids[part].at[by - 1],
            send_sem=mid_send.at[part, by],
            recv_sem=mid_recv.at[part, by],
            device_id=place(moved(here, (part + 1) % 3, by), core),
            device_id_type=MESH,
        )

    def last_copy(part, by, step, flip, source):
        second, third = (part + 1) % 3, (part + 2) % 3
        target = moved(here, third, step)
        there_core = (core + flip) % 2
        rows = pl.ds(pl.multiple_of((target[third] * 2 + there_core) * PICK, PICK), PICK)
        origin = (here[second] + SIDE - by) % SIDE
        block = (here[third] * 2 + core) * SIDE + origin
        return source.at[rows], outs[part].at[block], target, there_core

    def last_remote(part, by, index, source):
        step, flip = index // 2, index % 2
        src, dst, target, there_core = last_copy(part, by, step, flip, source)
        return pltpu.make_async_remote_copy(
            src_ref=src,
            dst_ref=dst,
            send_sem=last_send.at[part, by, index],
            recv_sem=last_recv.at[part, by, index],
            device_id=place(target, there_core),
            device_id_type=MESH,
        )

    def last_local(part, by, source):
        src, dst, _, _ = last_copy(part, by, 0, 0, source)
        return pltpu.make_async_copy(src, dst, last_recv.at[part, by, 0])

    def forward(part, by, source):
        last_local(part, by, source).start()

        def body(index, carry):
            last_remote(part, by, index, source).start()
            return carry

        lax.fori_loop(1, 8, body, 0)

    row = lax.broadcasted_iota(jnp.int32, (PICK, 512), 0)
    lane = lax.broadcasted_iota(jnp.int32, (PICK, 512), 1)
    wanted = jnp.where(lane // 128 == row // CAP, row % CAP, -7).astype(jnp.float32)

    for part in range(3):
        own_line(part).wait()
        own_table(part).wait()
        for by in (1, 3, 2):
            line_copy(part, by).wait()
            table_copy(part, by).wait()

    for part in range(3):

        def select(i, carry, part=part):
            by = (i + 1) % SIDE
            target = (here[(part + 1) % 3] + by) % SIDE
            first = pl.multiple_of(target * 8, 8)
            ranks = jnp.concatenate(
                [got_tables[part, s, pl.ds(first, 8), :] for s in range(SIDE)], axis=1
            )
            helds = jnp.concatenate(
                [got_tables[part, s, pl.ds(first + 32, 8), :] for s in range(SIDE)], axis=1
            )
            scales = []
            for j in range(8):
                hit = ranks[j : j + 1, :] == wanted
                picks[pl.ds(j * PICK, PICK), :] = jnp.where(hit, 1.0, 0.0).astype(jnp.bfloat16)
                scales.append(
                    jnp.sum(jnp.where(hit, helds[j : j + 1, :], 0.0), axis=1, keepdims=True)
                )
            factor = jnp.concatenate(scales, axis=0)
            for start in range(0, WIDTHS[part], 256):
                width = min(256, WIDTHS[part] - start)
                found = jnp.dot(
                    picks[...],
                    lines[part][:, start : start + width],
                    preferred_element_type=jnp.float32,
                )
                sends[part][by, :, start : start + width] = (found * factor).astype(jnp.bfloat16)

            @pl.when(by > 0)
            def _():
                mid_copy(part, by).start()

            return carry

        lax.fori_loop(0, SIDE, select, 0)
        forward(part, 0, sends[part].at[0])

    for by in (1, 2, 3):
        for part in range(3):
            mid_copy(part, by).wait()
            forward(part, by, mids[part].at[by - 1])

    for part in range(3):

        def finish(i, carry, part=part):
            last_local(part, i, sends[part].at[0]).wait()

            def body(index, inner):
                last_remote(part, i, index, sends[part].at[0]).wait()
                return inner

            return lax.fori_loop(1, 8, body, carry)

        lax.fori_loop(0, SIDE, finish, 0)


def dispatch(route_t, gate_t, rollout_ids, advantages, out_grad):
    vmem = pl.BlockSpec(memory_space=pltpu.VMEM)
    scratch = [pltpu.VMEM((512, w), jnp.bfloat16) for w in WIDTHS]
    scratch += [
        pltpu.VMEM((3, SIDE, 64, 128), jnp.float32),
        pltpu.VMEM((3, SIDE, 64, 128), jnp.float32),
        pltpu.VMEM((8 * PICK, 512), jnp.bfloat16),
    ]
    scratch += [pltpu.VMEM((SIDE, 8 * PICK, w), jnp.bfloat16) for w in WIDTHS]
    scratch += [pltpu.VMEM((SIDE - 1, 8 * PICK, w), jnp.bfloat16) for w in WIDTHS]
    scratch += [pltpu.SemaphoreType.DMA((6,))]
    scratch += [pltpu.SemaphoreType.DMA((3, SIDE)) for _ in range(6)]
    scratch += [pltpu.SemaphoreType.DMA((3, SIDE, 8)) for _ in range(2)]
    return pl.pallas_call(
        dispatch_kernel,
        out_shape=[jax.ShapeDtypeStruct((32, PICK, w), jnp.bfloat16) for w in WIDTHS],
        in_specs=[vmem] * 5,
        out_specs=[pl.BlockSpec(memory_space=pl.ANY)] * 3,
        scratch_shapes=scratch,
        compiler_params=pltpu.CompilerParams(
            collective_id=0, has_side_effects=True, vmem_limit_bytes=50 << 20
        ),
    )(route_t, gate_t, rollout_ids, advantages, out_grad)


def ordered(rows, part):
    width = rows.shape[-1]
    names = ("zh", "c", "y", "x", "zl")
    grid = rows.reshape(2, 2, 4, 4, 2, CAP, width)
    at = {n: i for i, n in enumerate(names)}
    axes = {"x": ["x"], "y": ["y"], "z": ["zh", "zl"]}
    order = "xyz"
    first, second, third = (order[(part + i) % 3] for i in range(3))
    want = axes[third] + ["c"] + axes[second] + axes[first]
    return grid.transpose([at[n] for n in want] + [5, 6]).reshape(1536, width)


def unordered(rows, part):
    width = rows.shape[-1]
    names = ["zh", "c", "y", "x", "zl"]
    size = {"zh": 2, "c": 2, "y": 4, "x": 4, "zl": 2}
    axes = {"x": ["x"], "y": ["y"], "z": ["zh", "zl"]}
    order = "xyz"
    first, second, third = (order[(part + i) % 3] for i in range(3))
    have = axes[third] + ["c"] + axes[second] + axes[first]
    grid = rows.reshape([size[n] for n in have] + [CAP, width])
    return grid.transpose([have.index(n) for n in names] + [5, 6]).reshape(1536, width)


def shards(hidden, out_grad, route_ids, gate_vals, rollout_ids, advantages, down_weight):
    slots = 1024
    flat_ids = route_ids.reshape(slots)
    named = jnp.sum(
        (route_ids[:, :, None] == jnp.arange(128, dtype=jnp.int32)).astype(jnp.bfloat16), axis=1
    )
    t = jnp.arange(128, dtype=jnp.int32)
    earlier = (t[:, None] > t[None, :]).astype(jnp.bfloat16)
    before = jnp.dot(earlier, named, preferred_element_type=jnp.float32)
    rank = jnp.sum(
        jnp.where(
            route_ids[:, :, None] == jnp.arange(128, dtype=jnp.int32), before[:, None, :], 0.0
        ),
        axis=2,
    ).astype(jnp.int32)
    spot = (route_ids * CAP + rank).reshape(slots)
    one_hot = (jnp.arange(1536, dtype=jnp.int32)[:, None] == spot[None, :]).astype(jnp.bfloat16)

    parts = dispatch(route_ids.T, gate_vals.T, rollout_ids, advantages, out_grad)
    hidden_send = jnp.dot(
        one_hot, hidden.reshape(slots, 768), preferred_element_type=jnp.float32
    ).astype(jnp.bfloat16)

    def exchange(rows):
        rows = rows.reshape(128, 24, 384)
        rows = lax.all_to_all(rows, ("grp", "ep"), split_axis=0, concat_axis=0, tiled=True)
        return rows.reshape(1536, 768)

    got_hidden = exchange(hidden_send)
    weight = down_weight[0]
    grads = []
    answers = jnp.zeros((1536, 768), jnp.float32)
    for part in range(3):
        got = parts[part].reshape(1536, WIDTHS[part])
        grads.append(
            lax.dot_general(
                ordered(got_hidden, part),
                got,
                (((0,), (0,)), ((), ())),
                preferred_element_type=jnp.float32,
            ).astype(jnp.bfloat16)
        )
        answer = lax.dot_general(
            got,
            weight[:, STARTS[part] : STARTS[part] + WIDTHS[part]],
            (((1,), (1,)), ((), ())),
            preferred_element_type=jnp.float32,
        )
        answers = answers + unordered(answer, part)
    weight_grad = jnp.concatenate(grads, axis=1)
    returned = exchange(answers.astype(jnp.bfloat16))
    hidden_grad = lax.dot_general(
        one_hot, returned, (((0,), (0,)), ((), ())), preferred_element_type=jnp.float32
    ).astype(jnp.bfloat16)
    return hidden_grad.reshape(128, 8, 768), weight_grad[None]


def solution(mesh):
    wide = P(("grp", "ep"), None, None)
    flat = P(("grp", "ep"), None)
    return jax.shard_map(
        shards,
        mesh=mesh,
        in_specs=(wide, flat, flat, flat, flat, flat, wide),
        out_specs=(wide, wide),
        check_vma=False,
    )
```

time: 452 us -> 285 us (0.63)
  waiting for transfers between devices: 252 us -> 8.52 us
  Pallas kernels: 0 us -> 148 us
  local copies, waits for them, and re-layouts: 100 us -> 59.8 us
  starting transfers between devices: 40.1 us -> 18 us
  other arithmetic: 10.4 us -> 4.51 us
    all_to_all x3 -> x2, waiting for transfers between devices: 252 us -> 8.52 us  [exchange(): lax.all_to_all(rows, ('grp', 'ep'), split_axis=0, concat_axis=0, tiled=True)]
    pallas_call x0 -> x1, Pallas kernels: none -> 148 us  [dispatch(): pl.pallas_call(dispatch_kernel, out_shape=[jax.ShapeDtypeStruct((32, PICK...]
    gather x3 -> x0, local copies, waits for them, and re-layouts: 37.4 us -> none  [the longest x1 26.5 us: shards(): scaled_send = scaled_pad[source]]
    reshape x5, local copies, waits for them, and re-layouts: 49.4 us -> 23.3 us  [the longest x3 14.8 us: ordered(): return grid.transpose([at[n] for n in want] + [5, 6]).reshape(1536, width)]
    dot_general x0 -> x3, local copies, waits for them, and re-layouts: none -> 22.8 us  [shards(): lax.dot_general(got, weight[:, STARTS[part]:STARTS[part] + WIDTHS[part]],...]
    all_to_all x3 -> x2, starting transfers between devices: 40.1 us -> 18 us  [exchange(): lax.all_to_all(rows, ('grp', 'ep'), split_axis=0, concat_axis=0, tiled=True)]
    concatenate x2 -> x0, local copies, waits for them, and re-layouts: 7.82 us -> none  [the longest x1 7.72 us: shards(): jnp.concatenate([scaled, jnp.zeros((1, model_width), jnp.bfloat16)], axis=0)]
    convert_element_type x3 -> x0, other arithmetic: 6.8 us -> none  [the longest x1 5.37 us: shards(): (slot_scale[:, :, None] * out_grad[:, None, :].astype(jnp.float32)).astyp...]
  transfers between devices with their start and end apart: 3 -> 2, of which waited for: 3 -> 1; matrix products, arithmetic and copies ran while one was open for 18% -> 26% of each run, Pallas kernels for 0% -> 52%
where the time goes in v1:
time: 285 us; the launch traced here: 284 us
  Pallas kernels  148 us (52%)
  local copies, waits for them, and re-layouts  59.8 us (21%)
  matrix products  43.7 us (15%)
  starting transfers between devices  18 us (6%)
  waiting for transfers between devices  8.52 us (3%)
  other arithmetic  4.51 us (2%)
    pallas_call x1, Pallas kernels, dispatch(): pl.pallas_call(dispatch_kernel, out_shape=[jax.ShapeDtypeStruct((32, PICK...  148 us
    dot_general x3, matrix products, shards(): lax.dot_general(got, weight[:, STARTS[part]:STARTS[part] + WIDTHS[part]],...  23.9 us
    dot_general x3, local copies, waits for them, and re-layouts, shards(): lax.dot_general(got, weight[:, STARTS[part]:STARTS[part] + WIDTHS[part]],...  22.8 us
    all_to_all x2, starting transfers between devices, exchange(): lax.all_to_all(rows, ('grp', 'ep'), split_axis=0, concat_axis=0, tiled=True)  18 us
    reshape x3, local copies, waits for them, and re-layouts, ordered(): return grid.transpose([at[n] for n in want] + [5, 6]).reshape(1536, width)  14.8 us
    dot_general x3, matrix products, shards(): lax.dot_general(ordered(got_hidden, part), got, (((0,), (0,)), ((), ())),...  11.6 us
    all_to_all x2, waiting for transfers between devices, exchange(): lax.all_to_all(rows, ('grp', 'ep'), split_axis=0, concat_axis=0, tiled=True)  8.52 us
    transpose x3, local copies, waits for them, and re-layouts, ordered(): return grid.transpose([at[n] for n in want] + [5, 6]).reshape(1536, width)  6.14 us
  transfers between devices with their start and end apart: 2, of which 1 were waited for; matrix products, arithmetic and copies ran while one was open for 26% of the time, Pallas kernels for 52%

profile of v1, /device:TPU:1, one launch (start us, length us, event | category | flops | bytes accessed | tf_op | source)
XLA Modules:
  0.0 283.7 jit_solution(9167243283272096553)
XLA Ops:
  0.6 0.9 copy.39
  1.6 0.2 fusion.14
  1.8 0.1 fusion.15
  1.9 0.4 select_reduce_fusion
  2.4 0.7 convert_add_fusion
  3.3 4.0 %fusion.7 = bf16[1536,768]{1,0:T(8,128)(2,1)} fusion(s32[1024]{0:T(1024)S(1)} %eq.18, bf16[128,8,768]{2,1,0:T(8,128)(2,1)S(1)} %copy-done), kind=kOutput, calls=%fused_computation.11 | convolution fusion | flops 2418671616 | bytes 3936256 | tf_op jit(solution)/shard_map/dot_general | solution.py:347
  7.3 4.9 %reshape.63 = bf16[128,24,384]{2,1,0:T(8,128)(2,1)} reshape(bf16[1536,768]{1,0:T(8,128)(2,1)} %fusion.7) | data formatting | bytes 4718592 | tf_op jit(solution)/shard_map/reshape | solution.py:352
  12.2 11.9 %all-to-all-start.1 = ((bf16[128,24,384]{2,1,0:T(8,128)(2,1)}), bf16[128,24,384]{2,1,0:T(8,128)(2,1)}, u32[]{:S(2)}, u32[]{:S(2)}) async-start(bf16[128,24,384]{2,1,0:T(8,128)(2,1)} %reshape.63), calls=%async_computation.1 | async-start | bytes 4718592 | tf_op jit(solution)/shard_map/all_to_all | solution.py:353
  24.2 148.3 %shard_map.86 = (bf16[32,48,1408]{2,1,0:T(8,128)(2,1)}, bf16[32,48,1408]{2,1,0:T(8,128)(2,1)}, bf16[32,48,1280]{2,1,0:T(8,128)(2,1)}) custom-call(s32[8,128]{1,0:T(8,128)S(1)} %bitcast.50, f32[8,128]{1,0:T(8,128)S(1)} %bitcast.51, s32[1,128]{1,0:T(1,128)S(1)} %copy-done.5, f32[1,4]{1,0:T(1,128)S(1)} %copy-done.6, bf16[128,4096]{1,0:T(8,128)(2,1)S(1)} %copy-done.2), custom_call_target="tpu_custom_call" | custom-call | tf_op jit(solution)/shard_map/pallas_call | solution.py:292
  172.5 7.9 %reshape.74 = bf16[4,2,2,2,4,12,1408]{6,5,4,3,2,1,0:T(8,128)(2,1)} reshape(bf16[32,48,1408]{2,1,0:T(8,128)(2,1)} %get-tuple-element.6) | data formatting | bytes 8650752 | tf_op jit(solution)/shard_map/dot_general | solution.py:370
  180.3 7.0 %reshape.75 = bf16[4,2,4,2,2,12,1280]{6,5,4,3,2,1,0:T(8,128)(2,1)} reshape(bf16[32,48,1280]{2,1,0:T(8,128)(2,1)} %get-tuple-element.7) | data formatting | bytes 7864320 | tf_op jit(solution)/shard_map/dot_general | solution.py:370
  187.3 8.0 %reshape.73 = bf16[2,2,2,4,4,12,1408]{6,5,4,3,2,1,0:T(8,128)(2,1)} reshape(bf16[32,48,1408]{2,1,0:T(8,128)(2,1)} %get-tuple-element.5) | data formatting | bytes 8650752 | tf_op jit(solution)/shard_map/dot_general | solution.py:370
  195.3 7.9 %fusion.3 = f32[4,2,2,2,4,12,768]{6,5,0,4,1,3,2:T(8,128)S(1)} fusion(bf16[4,2,2,2,4,12,1408]{6,5,4,3,2,1,0:T(8,128)(2,1)} %reshape.74, bf16[768,4096]{1,0:T(8,128)(2,1)} %bitcast.64), kind=kOutput, calls=%fused_computation.7 | convolution fusion | flops 3321888768 | bytes 12648448 | tf_op jit(solution)/shard_map/dot_general | solution.py:370
  203.3 7.8 %fusion.5 = f32[4,2,4,2,2,12,768]{6,5,2,0,1,4,3:T(8,128)} fusion(bf16[4,2,4,2,2,12,1280]{6,5,4,3,2,1,0:T(8,128)(2,1)S(1)} %bitcast.56, bf16[768,4096]{1,0:T(8,128)(2,1)} %bitcast.65), kind=kOutput, calls=%fused_computation.9 | convolution fusion | flops 3019898880 | bytes 10616832 | tf_op jit(solution)/shard_map/dot_general | solution.py:370
  211.1 8.1 %fusion = bf16[2,2,4,4,2,12,768]{6,5,3,2,1,4,0:T(8,128)(2,1)S(1)} fusion(f32[4,2,4,2,2,12,768]{6,5,2,0,1,4,3:T(8,128)} %fusion.5, f32[4,2,2,2,4,12,768]{6,5,0,4,1,3,2:T(8,128)S(1)} %fusion.3, bf16[2,2,2,4,4,12,1408]{6,5,4,3,2,1,0:T(8,128)(2,1)S(1)} %copy-done.7, bf16[768,4096]{1,0:T(8,128)(2,1)} %bitcast.66), kind=kOutput, calls=%fused_computation.2 | convolution fusion | flops 3325427712 | bytes 19857408 | tf_op jit(solution)/shard_map/dot_general | solution.py:370
  219.2 0.4 copy.48
  219.6 2.3 convert_element_type.35
  221.9 6.1 %all-to-all-start = ((bf16[128,24,384]{2,1,0:T(8,128)(2,1)}), bf16[128,24,384]{2,1,0:T(8,128)(2,1)}, u32[]{:S(2)}, u32[]{:S(2)}) async-start(bf16[128,24,384]{2,1,0:T(8,128)(2,1)} %convert_element_type.35), calls=%async_computation | async-start | bytes 4718592 | tf_op jit(solution)/shard_map/all_to_all | solution.py:353
  228.0 3.6 %reshape_reshape.2 = bf16[2,2,4,4,2,12,768]{6,5,4,3,2,1,0:T(8,128)(2,1)S(1)} reshape(bf16[128,24,384]{2,1,0:T(8,128)(2,1)} %all-to-all-done.1) | data formatting | bytes 4718592 | tf_op jit(solution)/shard_map/reshape;reshape | solution.py:307
  231.6 2.1 copy.50
  233.7 5.0 %reshape.66 = bf16[1536,768]{1,0:T(8,128)(2,1)} reshape(bf16[4,2,2,2,4,12,768]{6,5,4,3,2,1,0:T(8,128)(2,1)} %copy.50) | data formatting | bytes 4718592 | tf_op jit(solution)/shard_map/reshape | solution.py:313
  238.7 2.1 copy.49
  240.8 4.9 %reshape.64 = bf16[1536,768]{1,0:T(8,128)(2,1)} reshape(bf16[2,2,2,4,4,12,768]{6,5,4,3,2,1,0:T(8,128)(2,1)} %copy.49) | data formatting | bytes 4718592 | tf_op jit(solution)/shard_map/reshape | solution.py:313
  245.7 1.9 copy.51
  247.6 4.9 %reshape.68 = bf16[1536,768]{1,0:T(8,128)(2,1)} reshape(bf16[4,2,4,2,2,12,768]{6,5,4,3,2,1,0:T(8,128)(2,1)} %copy.51) | data formatting | bytes 4718592 | tf_op jit(solution)/shard_map/reshape | solution.py:313
  252.6 8.5 %all-to-all-done = bf16[128,24,384]{2,1,0:T(8,128)(2,1)} async-done(((bf16[128,24,384]{2,1,0:T(8,128)(2,1)}), bf16[128,24,384]{2,1,0:T(8,128)(2,1)}, u32[]{:S(2)}, u32[]{:S(2)}) %all-to-all-start) | async-done | bytes 2359328 | tf_op jit(solution)/shard_map/all_to_all | solution.py:353
  261.1 3.6 %reshape.60 = bf16[1536,768]{1,0:T(8,128)(2,1)S(1)} reshape(bf16[128,24,384]{2,1,0:T(8,128)(2,1)} %all-to-all-done) | data formatting | bytes 4718592 | tf_op jit(solution)/shard_map/reshape | solution.py:354
  264.7 4.2 %fusion.12 = bf16[128,8,768]{2,1,0:T(8,128)(2,1)} fusion(bf16[1536,768]{1,0:T(8,128)(2,1)S(1)} %reshape.60, s32[1024]{0:T(1024)S(1)} %eq.18), kind=kOutput, calls=%fused_computation.22 | convolution fusion | flops 2418278400 | bytes 3936256 | tf_op jit(solution)/shard_map/dot_general | solution.py:379
  268.9 4.1 %convolution_convert_fusion.1 = bf16[768,1408]{1,0:T(8,128)(2,1)S(1)} fusion(bf16[1536,768]{1,0:T(8,128)(2,1)S(1)} %copy-done.9, bf16[1536,1408]{1,0:T(8,128)(2,1)S(1)} %bitcast.62), kind=kOutput, calls=%fused_computation.13 | convolution fusion | flops 3322970112 | bytes 8847360 | tf_op jit(solution)/shard_map/dot_general | solution.py:363
  273.0 4.1 %convolution_convert_fusion.2 = bf16[768,1408]{1,0:T(8,128)(2,1)S(1)} fusion(bf16[1536,768]{1,0:T(8,128)(2,1)S(1)} %copy-done.10, bf16[1536,1408]{1,0:T(8,128)(2,1)S(1)} %bitcast.59), kind=kOutput, calls=%fused_computation.14 | convolution fusion | flops 3322970112 | bytes 8847360 | tf_op jit(solution)/shard_map/dot_general | solution.py:363
  277.2 3.4 %convolution_convert_fusion = bf16[768,1280]{1,0:T(8,128)(2,1)S(1)} fusion(bf16[1536,768]{1,0:T(8,128)(2,1)S(1)} %copy-done.11, bf16[1536,1280]{1,0:T(8,128)(2,1)S(1)} %bitcast.63), kind=kOutput, calls=%fused_computation.12 | convolution fusion | flops 3020881920 | bytes 8257536 | tf_op jit(solution)/shard_map/dot_general | solution.py:363
  280.5 3.2 %maximum_bitcast_fusion = bf16[1,768,4096]{2,1,0:T(8,128)(2,1)} fusion(bf16[768,1280]{1,0:T(8,128)(2,1)S(1)} %convolution_convert_fusion, bf16[768,1408]{1,0:T(8,128)(2,1)S(1)} %convolution_convert_fusion.1, bf16[768,1408]{1,0:T(8,128)(2,1)S(1)} %convolution_convert_fusion.2), kind=kLoop, calls=%fused_computation | loop fusion | flops 18874368 | bytes 12582912 | tf_op jit(solution)/shard_map/broadcast_in_dim | solution.py:382
  (43 shorter events, 0.3 us)
Async XLA Ops:
  0.6 2.6 copy-start
  7.3 16.8 %copy-start.2 = (bf16[128,4096]{1,0:T(8,128)(2,1)S(1)}, bf16[128,4096]{1,0:T(8,128)(2,1)}, u32[]{:S(2)}) copy-start(bf16[128,4096]{1,0:T(8,128)(2,1)} %grad_ref.1) | copy-start | bytes 3145732
  7.3 16.8 %copy-start.3 = (s32[128,8]{0,1:T(8,128)S(1)}, s32[128,8]{0,1:T(8,128)}, u32[]{:S(2)}) copy-start(s32[128,8]{0,1:T(8,128)} %param.9) | copy-start | bytes 12292
  7.3 16.9 %copy-start.4 = (f32[128,8]{0,1:T(8,128)S(1)}, f32[128,8]{0,1:T(8,128)}, u32[]{:S(2)}) copy-start(f32[128,8]{0,1:T(8,128)} %param.10) | copy-start | bytes 12292
  7.3 16.9 %copy-start.5 = (s32[1,128]{1,0:T(1,128)S(1)}, s32[1,128]{1,0:T(1,128)}, u32[]{:S(2)}) copy-start(s32[1,128]{1,0:T(1,128)} %rollout_ref.1) | copy-start | bytes 1540
  7.3 16.9 %copy-start.6 = (f32[1,4]{1,0:T(1,128)S(1)}, f32[1,4]{1,0:T(1,128)}, u32[]{:S(2)}) copy-start(f32[1,4]{1,0:T(1,128)} %adv_ref.1) | copy-start | bytes 52
  12.2 209.7 %all-to-all-start.1 = ((bf16[128,24,384]{2,1,0:T(8,128)(2,1)}), bf16[128,24,384]{2,1,0:T(8,128)(2,1)}, u32[]{:S(2)}, u32[]{:S(2)}) async-start(bf16[128,24,384]{2,1,0:T(8,128)(2,1)} %reshape.63), calls=%async_computation.1 | async-start | bytes 4718592 | tf_op jit(solution)/shard_map/all_to_all | solution.py:353
  187.3 15.9 %slice-start = ((s8[5242880]{0:T(1024)(128)(4,1)}), s8[1048576]{0:T(1024)(128)(4,1)S(1)}, s32[]{:S(2)}) async-start(s8[5242880]{0:T(1024)(128)(4,1)} %bitcast.55), calls=%async_computation.2 | async-start | bytes 2097152
  195.3 7.9 %slice-start.1 = ((s8[5242880]{0:T(1024)(128)(4,1)}), s8[4194304]{0:T(1024)(128)(4,1)S(1)}, s32[]{:S(2)}) async-start(s8[5242880]{0:T(1024)(128)(4,1)} %bitcast.55), calls=%async_computation.3 | async-start | bytes 8388608
  203.2 7.9 %copy-start.7 = (bf16[2,2,2,4,4,12,1408]{6,5,4,3,2,1,0:T(8,128)(2,1)S(1)}, bf16[2,2,2,4,4,12,1408]{6,5,4,3,2,1,0:T(8,128)(2,1)}, u32[]{:S(2)}) copy-start(bf16[2,2,2,4,4,12,1408]{6,5,4,3,2,1,0:T(8,128)(2,1)} %reshape.73) | copy-start | bytes 12976132
  221.9 39.2 %all-to-all-start = ((bf16[128,24,384]{2,1,0:T(8,128)(2,1)}), bf16[128,24,384]{2,1,0:T(8,128)(2,1)}, u32[]{:S(2)}, u32[]{:S(2)}) async-start(bf16[128,24,384]{2,1,0:T(8,128)(2,1)} %convert_element_type.35), calls=%async_computation | async-start | bytes 4718592 | tf_op jit(solution)/shard_map/all_to_all | solution.py:353
  261.1 7.7 %slice-start.4 = ((s8[4325376]{0:T(1024)(128)(4,1)}), s8[131072]{0:T(1024)(128)(4,1)S(1)}, s32[]{:S(2)}) async-start(s8[4325376]{0:T(1024)(128)(4,1)} %bitcast.60), calls=%async_computation.6 | async-start | bytes 262144
  264.6 4.2 %slice-start.5 = ((s8[4325376]{0:T(1024)(128)(4,1)}), s8[4194304]{0:T(1024)(128)(4,1)S(1)}, s32[]{:S(2)}) async-start(s8[4325376]{0:T(1024)(128)(4,1)} %bitcast.60), calls=%async_computation.7 | async-start | bytes 8388608
  264.7 4.2 %copy-start.9 = (bf16[1536,768]{1,0:T(8,128)(2,1)S(1)}, bf16[1536,768]{1,0:T(8,128)(2,1)}, u32[]{:S(2)}) copy-start(bf16[1536,768]{1,0:T(8,128)(2,1)} %reshape.66) | copy-start | bytes 7077892
  264.7 8.3 %slice-start.2 = ((s8[4325376]{0:T(1024)(128)(4,1)}), s8[4194304]{0:T(1024)(128)(4,1)S(1)}, s32[]{:S(2)}) async-start(s8[4325376]{0:T(1024)(128)(4,1)} %bitcast.57), calls=%async_computation.4 | async-start | bytes 8388608
  268.8 4.1 %slice-start.3 = ((s8[4325376]{0:T(1024)(128)(4,1)}), s8[131072]{0:T(1024)(128)(4,1)S(1)}, s32[]{:S(2)}) async-start(s8[4325376]{0:T(1024)(128)(4,1)} %bitcast.57), calls=%async_computation.5 | async-start | bytes 262144
  268.9 4.1 %copy-start.10 = (bf16[1536,768]{1,0:T(8,128)(2,1)S(1)}, bf16[1536,768]{1,0:T(8,128)(2,1)}, u32[]{:S(2)}) copy-start(bf16[1536,768]{1,0:T(8,128)(2,1)} %reshape.64) | copy-start | bytes 7077892
  273.0 4.1 %copy-start.8 = (bf16[32,48,1280]{2,1,0:T(8,128)(2,1)S(1)}, bf16[32,48,1280]{2,1,0:T(8,128)(2,1)}, u32[]{:S(2)}) copy-start(bf16[32,48,1280]{2,1,0:T(8,128)(2,1)} %get-tuple-element.7) | copy-start | bytes 11796484
  273.0 4.1 %copy-start.11 = (bf16[1536,768]{1,0:T(8,128)(2,1)S(1)}, bf16[1536,768]{1,0:T(8,128)(2,1)}, u32[]{:S(2)}) copy-start(bf16[1536,768]{1,0:T(8,128)(2,1)} %reshape.68) | copy-start | bytes 7077892
  277.2 6.6 %copy-start.1 = (bf16[128,8,768]{2,1,0:T(8,128)(2,1)S(1)}, bf16[128,8,768]{2,1,0:T(8,128)(2,1)}, u32[]{:S(2)}) copy-start(bf16[128,8,768]{2,1,0:T(8,128)(2,1)} %param.7) | copy-start | bytes 4718596

commit v2 on v1

--- a/solution.py
+++ b/solution.py
@@ -11,8 +11,8 @@
 SIDE = 4
 CAP = 12
 PICK = SIDE * CAP
-WIDTHS = (1408, 1408, 1280)
-STARTS = (0, 1408, 2816)
+WIDTHS = (1280, 1280, 1536)
+STARTS = (0, 1280, 2560)
 
 
 def position():
@@ -51,6 +51,14 @@
     rollout_ref,
     adv_ref,
     grad_ref,
+    weight_ref,
+    kept0,
+    kept1,
+    kept2,
+    answer_ref,
+    weight,
+    total,
+    answer,
     out0,
     out1,
     out2,
@@ -67,6 +75,7 @@
     mid1,
     mid2,
     local_sem,
+    keep_sem,
     line_send,
     line_recv,
     table_send,
@@ -77,6 +86,7 @@
     last_recv,
 ):
     outs, lines = (out0, out1, out2), (lines0, lines1, lines2)
+    kept = (kept0, kept1, kept2)
     sends, mids = (send0, send1, send2), (mid0, mid1, mid2)
     here, core = position()
 
@@ -132,14 +142,16 @@
             line_copy(part, by).start()
     for part in range(3):
         own_line(part).start()
+    load_weight = pltpu.make_async_copy(weight_ref.at[0], weight, local_sem.at[6])
+    load_weight.start()
 
     rollout = rollout_ref[...]
-    weight = jnp.zeros((1, 128), jnp.float32)
+    token_weight = jnp.zeros((1, 128), jnp.float32)
     for i in range(4):
         hit = (rollout == i).astype(jnp.float32)
         count = jnp.sum(hit, axis=1, keepdims=True)
-        weight = weight + hit * (adv_ref[:, i : i + 1] * 32.0 / count)
-    scale = gate_ref[...] * weight
+        token_weight = token_weight + hit * (adv_ref[:, i : i + 1] * 32.0 / count)
+    scale = gate_ref[...] * token_weight
     route = route_ref[...]
     sooner = (
         lax.broadcasted_iota(jnp.int32, (128, 128), 0)
@@ -180,8 +192,8 @@
         there_core = (core + flip) % 2
         rows = pl.ds(pl.multiple_of((target[third] * 2 + there_core) * PICK, PICK), PICK)
         origin = (here[second] + SIDE - by) % SIDE
-        block = (here[third] * 2 + core) * SIDE + origin
-        return source.at[rows], outs[part].at[block], target, there_core
+        block = here[third] * 2 + core
+        return source.at[rows], outs[part].at[block, origin], target, there_core
 
     def last_remote(part, by, index, source):
         step, flip = index // 2, index % 2
@@ -257,28 +269,91 @@
         lax.fori_loop(0, SIDE, select, 0)
         forward(part, 0, sends[part].at[0])
 
-    for by in (1, 2, 3):
+    def keep(part, by):
+        origin = (here[(part + 1) % 3] + SIDE - by) % SIDE
+        return pltpu.make_async_copy(
+            outs[part].at[:, origin], kept[part].at[:, origin], keep_sem.at[part, by]
+        )
+
+    def absorb(part, by):
+        last_local(part, by, mids[part].at[0]).wait()
+
+        def arrive(index, carry):
+            last_remote(part, by, index, mids[part].at[0]).wait_recv()
+            return carry
+
+        lax.fori_loop(1, 8, arrive, 0)
+        keep(part, by).start()
+        origin = (here[(part + 1) % 3] + SIDE - by) % SIDE
+        rows = outs[part][:, origin].reshape(8 * PICK, WIDTHS[part])
+        product = lax.dot_general(
+            rows,
+            weight[:, STARTS[part] : STARTS[part] + WIDTHS[part]],
+            (((1,), (1,)), ((), ())),
+            preferred_element_type=jnp.float32,
+        )
+        for block in range(8):
+            for j in range(SIDE):
+                coords = [None] * 3
+                coords[part] = j
+                coords[(part + 1) % 3] = origin
+                coords[(part + 2) % 3] = block // 2
+                group, owner = place(coords, block % 2)
+                first = block * PICK + j * CAP
+                device = group * 32 + owner
+                total[device] = total[device] + product[first : first + CAP]
+
+    total[...] = jnp.zeros_like(total)
+    load_weight.wait()
+
+    def onward(step, carry):
+        @pl.when(step < SIDE)
+        def _():
+            for part in range(3):
+                mid_copy(part, step).wait()
+                forward(part, step, mids[part].at[step - 1])
+
         for part in range(3):
-            mid_copy(part, by).wait()
-            forward(part, by, mids[part].at[by - 1])
+            absorb(part, step - 1)
+        return carry
+
+    lax.fori_loop(1, SIDE + 1, onward, 0)
+
+    def pack(device, carry):
+        rows = total[device]
+        rows = jnp.concatenate([rows[:, :384], rows[:, 384:]], axis=0)
+        answer[device] = rows.astype(jnp.bfloat16)
+        return carry
+
+    lax.fori_loop(0, 128, pack, 0)
+    give = pltpu.make_async_copy(answer, answer_ref, local_sem.at[7])
+    give.start()
 
     for part in range(3):
 
         def finish(i, carry, part=part):
-            last_local(part, i, sends[part].at[0]).wait()
+            keep(part, i).wait()
 
             def body(index, inner):
-                last_remote(part, i, index, sends[part].at[0]).wait()
+                last_remote(part, i, index, mids[part].at[0]).wait_send()
                 return inner
 
             return lax.fori_loop(1, 8, body, carry)
 
         lax.fori_loop(0, SIDE, finish, 0)
-
-
-def dispatch(route_t, gate_t, rollout_ids, advantages, out_grad):
+    give.wait()
+
+
+def dispatch(route_t, gate_t, rollout_ids, advantages, out_grad, down_weight):
     vmem = pl.BlockSpec(memory_space=pltpu.VMEM)
-    scratch = [pltpu.VMEM((512, w), jnp.bfloat16) for w in WIDTHS]
+    hbm = pl.BlockSpec(memory_space=pl.ANY)
+    scratch = [
+        pltpu.VMEM((768, 4096), jnp.bfloat16),
+        pltpu.VMEM((128, CAP, 768), jnp.float32),
+        pltpu.VMEM((128, 2 * CAP, 384), jnp.bfloat16),
+    ]
+    scratch += [pltpu.VMEM((8, SIDE, PICK, w), jnp.bfloat16) for w in WIDTHS]
+    scratch += [pltpu.VMEM((512, w), jnp.bfloat16) for w in WIDTHS]
     scratch += [
         pltpu.VMEM((3, SIDE, 64, 128), jnp.float32),
         pltpu.VMEM((3, SIDE, 64, 128), jnp.float32),
@@ -286,43 +361,55 @@
     ]
     scratch += [pltpu.VMEM((SIDE, 8 * PICK, w), jnp.bfloat16) for w in WIDTHS]
     scratch += [pltpu.VMEM((SIDE - 1, 8 * PICK, w), jnp.bfloat16) for w in WIDTHS]
-    scratch += [pltpu.SemaphoreType.DMA((6,))]
-    scratch += [pltpu.SemaphoreType.DMA((3, SIDE)) for _ in range(6)]
+    scratch += [pltpu.SemaphoreType.DMA((8,))]
+    scratch += [pltpu.SemaphoreType.DMA((3, SIDE)) for _ in range(7)]
     scratch += [pltpu.SemaphoreType.DMA((3, SIDE, 8)) for _ in range(2)]
+    shapes = [jax.ShapeDtypeStruct((8, SIDE, PICK, w), jnp.bfloat16) for w in WIDTHS]
+    shapes += [jax.ShapeDtypeStruct((128, 2 * CAP, 384), jnp.bfloat16)]
     return pl.pallas_call(
         dispatch_kernel,
-        out_shape=[jax.ShapeDtypeStruct((32, PICK, w), jnp.bfloat16) for w in WIDTHS],
-        in_specs=[vmem] * 5,
-        out_specs=[pl.BlockSpec(memory_space=pl.ANY)] * 3,
+        out_shape=shapes,
+        in_specs=[vmem] * 5 + [hbm],
+        out_specs=[hbm] * 4,
         scratch_shapes=scratch,
         compiler_params=pltpu.CompilerParams(
-            collective_id=0, has_side_effects=True, vmem_limit_bytes=50 << 20
+            collective_id=0, has_side_effects=True, vmem_limit_bytes=62 << 20
         ),
-    )(route_t, gate_t, rollout_ids, advantages, out_grad)
-
-
-def ordered(rows, part):
-    width = rows.shape[-1]
-    names = ("zh", "c", "y", "x", "zl")
-    grid = rows.reshape(2, 2, 4, 4, 2, CAP, width)
-    at = {n: i for i, n in enumerate(names)}
-    axes = {"x": ["x"], "y": ["y"], "z": ["zh", "zl"]}
-    order = "xyz"
-    first, second, third = (order[(part + i) % 3] for i in range(3))
-    want = axes[third] + ["c"] + axes[second] + axes[first]
-    return grid.transpose([at[n] for n in want] + [5, 6]).reshape(1536, width)
-
-
-def unordered(rows, part):
-    width = rows.shape[-1]
-    names = ["zh", "c", "y", "x", "zl"]
-    size = {"zh": 2, "c": 2, "y": 4, "x": 4, "zl": 2}
-    axes = {"x": ["x"], "y": ["y"], "z": ["zh", "zl"]}
-    order = "xyz"
-    first, second, third = (order[(part + i) % 3] for i in range(3))
-    have = axes[third] + ["c"] + axes[second] + axes[first]
-    grid = rows.reshape([size[n] for n in have] + [CAP, width])
-    return grid.transpose([have.index(n) for n in names] + [5, 6]).reshape(1536, width)
+    )(route_t, gate_t, rollout_ids, advantages, out_grad, down_weight)
+
+
+def arrange_kernel(got_ref, *out_refs):
+    for part in range(3):
+
+        def block_of(block, carry, part=part):
+            pieces = []
+            for j in range(SIDE):
+                coords = [None] * 3
+                coords[part] = j
+                coords[(part + 1) % 3] = block % SIDE
+                coords[(part + 2) % 3] = block // 8
+                group, owner = place(coords, (block // SIDE) % 2)
+                rows = got_ref[group * 32 + owner].astype(jnp.float32)
+                pieces.append(jnp.concatenate([rows[:CAP], rows[CAP:]], axis=1))
+            first = pl.multiple_of(block * PICK, PICK)
+            out_refs[part][pl.ds(first, PICK)] = jnp.concatenate(pieces, axis=0).astype(
+                jnp.bfloat16
+            )
+            return carry
+
+        lax.fori_loop(0, 32, block_of, 0)
+
+
+def arrange(got):
+    vmem = pl.BlockSpec(memory_space=pltpu.VMEM)
+    return pl.pallas_call(
+        arrange_kernel,
+        out_shape=[jax.ShapeDtypeStruct((1536, 768), jnp.bfloat16)] * 3,
+        in_specs=[vmem],
+        out_specs=[vmem] * 3,
+        compiler_params=pltpu.CompilerParams(vmem_limit_bytes=24 << 20),
+        cost_estimate=pl.CostEstimate(flops=0, bytes_accessed=10 << 20, transcendentals=0),
+    )(got)
 
 
 def shards(hidden, out_grad, route_ids, gate_vals, rollout_ids, advantages, down_weight):
@@ -343,39 +430,31 @@
     spot = (route_ids * CAP + rank).reshape(slots)
     one_hot = (jnp.arange(1536, dtype=jnp.int32)[:, None] == spot[None, :]).astype(jnp.bfloat16)
 
-    parts = dispatch(route_ids.T, gate_vals.T, rollout_ids, advantages, out_grad)
+    parts = dispatch(
+        route_ids.T, gate_vals.T, rollout_ids, advantages, out_grad, down_weight
+    )
     hidden_send = jnp.dot(
         one_hot, hidden.reshape(slots, 768), preferred_element_type=jnp.float32
     ).astype(jnp.bfloat16)
 
     def exchange(rows):
-        rows = rows.reshape(128, 24, 384)
-        rows = lax.all_to_all(rows, ("grp", "ep"), split_axis=0, concat_axis=0, tiled=True)
-        return rows.reshape(1536, 768)
-
-    got_hidden = exchange(hidden_send)
-    weight = down_weight[0]
-    grads = []
-    answers = jnp.zeros((1536, 768), jnp.float32)
-    for part in range(3):
-        got = parts[part].reshape(1536, WIDTHS[part])
-        grads.append(
-            lax.dot_general(
-                ordered(got_hidden, part),
-                got,
-                (((0,), (0,)), ((), ())),
-                preferred_element_type=jnp.float32,
-            ).astype(jnp.bfloat16)
-        )
-        answer = lax.dot_general(
-            got,
-            weight[:, STARTS[part] : STARTS[part] + WIDTHS[part]],
-            (((1,), (1,)), ((), ())),
+        return lax.all_to_all(rows, ("grp", "ep"), split_axis=0, concat_axis=0, tiled=True)
+
+    got_hidden = exchange(
+        hidden_send.reshape(128, CAP, 2, 384).transpose(0, 2, 1, 3).reshape(128, 2 * CAP, 384)
+    )
+    returned = exchange(parts[3])
+    grads = [
+        lax.dot_general(
+            rows,
+            part.reshape(1536, width),
+            (((0,), (0,)), ((), ())),
             preferred_element_type=jnp.float32,
-        )
-        answers = answers + unordered(answer, part)
+        ).astype(jnp.bfloat16)
+        for rows, part, width in zip(arrange(got_hidden), parts[:3], WIDTHS)
+    ]
     weight_grad = jnp.concatenate(grads, axis=1)
-    returned = exchange(answers.astype(jnp.bfloat16))
+    returned = returned.reshape(128, 2, CAP, 384).transpose(0, 2, 1, 3).reshape(1536, 768)
     hidden_grad = lax.dot_general(
         one_hot, returned, (((0,), (0,)), ((), ())), preferred_element_type=jnp.float32
     ).astype(jnp.bfloat16)

time: 285 us -> 239 us (0.84)
  local copies, waits for them, and re-layouts: 59.8 us -> 16 us
  waiting for transfers between devices: 8.52 us -> 41.3 us
  matrix products: 43.7 us -> 21.8 us
  starting transfers between devices: 18 us -> 9.98 us
  Pallas kernels: 148 us -> 145 us
    all_to_all x2, waiting for transfers between devices: 8.52 us -> 41.3 us  [exchange(): lax.all_to_all(rows, ('grp', 'ep'), split_axis=0, concat_axis=0, tiled=True)]
    dot_general x3 -> x0, local copies, waits for them, and re-layouts: 22.8 us -> none  [shards(): lax.dot_general(got, weight[:, STARTS[part]:STARTS[part] + WIDTHS[part]],...]
    dot_general x6 -> x3, matrix products: 35.4 us -> 13.4 us  [shards(): lax.dot_general(rows, part.reshape(1536, width), (((0,), (0,)), ((), ()))...]
    reshape x5 -> x3, local copies, waits for them, and re-layouts: 23.3 us -> 10.6 us  [shards(): hidden_send.reshape(128, CAP, 2, 384).transpose(0, 2, 1, 3)]
    all_to_all x2, starting transfers between devices: 18 us -> 9.98 us  [exchange(): lax.all_to_all(rows, ('grp', 'ep'), split_axis=0, concat_axis=0, tiled=True)]
    transpose x3 -> x1, local copies, waits for them, and re-layouts: 6.14 us -> 2.43 us  [shards(): returned.reshape(128, 2, CAP, 384).transpose(0, 2, 1, 3).reshape(1536, 768)]
    another operation x1 -> x0, local copies, waits for them, and re-layouts: 3.62 us -> none  [ordered(): grid = rows.reshape(2, 2, 4, 4, 2, CAP, width)]
    pallas_call x1 -> x2, Pallas kernels: 148 us -> 145 us  [the longest x1 140 us: dispatch(): pl.pallas_call(dispatch_kernel, out_shape=shapes, in_specs=[vmem] * 5 + [...]
  transfers between devices with their start and end apart: 2 -> 2, of which waited for: 1 -> 2; matrix products, arithmetic and copies ran while one was open for 26% -> 10% of each run, Pallas kernels for 52% -> 0%
where the time goes in v2:
time: 239 us
  Pallas kernels  145 us (61%)
  waiting for transfers between devices  41.3 us (17%)
  matrix products  21.8 us (9%)
  local copies, waits for them, and re-layouts  16 us (7%)
  starting transfers between devices  9.98 us (4%)
  other arithmetic  3.82 us (2%)
    pallas_call x1, Pallas kernels, dispatch(): pl.pallas_call(dispatch_kernel, out_shape=shapes, in_specs=[vmem] * 5 + [...  140 us
    all_to_all x2, waiting for transfers between devices, exchange(): lax.all_to_all(rows, ('grp', 'ep'), split_axis=0, concat_axis=0, tiled=True)  41.3 us
    dot_general x3, matrix products, shards(): lax.dot_general(rows, part.reshape(1536, width), (((0,), (0,)), ((), ()))...  13.4 us
    reshape x3, local copies, waits for them, and re-layouts, shards(): hidden_send.reshape(128, CAP, 2, 384).transpose(0, 2, 1, 3)  10.6 us
    all_to_all x2, starting transfers between devices, exchange(): lax.all_to_all(rows, ('grp', 'ep'), split_axis=0, concat_axis=0, tiled=True)  9.98 us
    pallas_call x1, Pallas kernels, arrange(): pl.pallas_call(arrange_kernel, out_shape=[jax.ShapeDtypeStruct((1536, 768...  5.3 us
  transfers between devices with their start and end apart: 2, of which 2 were waited for; matrix products, arithmetic and copies ran while one was open for 10% of the time, Pallas kernels for 0%

profile of v2, /device:TPU:1, one launch (start us, length us, event | category | flops | bytes accessed | tf_op | source)
XLA Modules:
  0.0 238.8 jit_solution(16470369608082598433)
XLA Ops:
  0.6 0.0 copy-start
  0.6 139.8 %shard_map.86 = (bf16[8,4,48,1280]{3,2,1,0:T(8,128)(2,1)}, bf16[8,4,48,1280]{3,2,1,0:T(8,128)(2,1)}, bf16[8,4,48,1536]{3,2,1,0:T(8,128)(2,1)}, bf16[128,24,384]{2,1,0:T(8,128)(2,1)}) custom-call(s32[8,128]{1,0:T(8,128)} %bitcast.33, f32[8,128]{1,0:T(8,128)} %bitcast.34, s32[1,128]{1,0:T(1,128)} %rollout_ref.1, f32[1,4]{1,0:T(1,128)} %adv_ref.1, ...), custom_call_target="tpu_custom_call" | custom-call | tf_op jit(solution)/shard_map/pallas_call | solution.py:369
  140.4 0.0 copy-start.1
  140.5 5.0 %all-to-all-start = ((bf16[128,24,384]{2,1,0:T(8,128)(2,1)}), bf16[128,24,384]{2,1,0:T(8,128)(2,1)}, u32[]{:S(2)}, u32[]{:S(2)}) async-start(bf16[128,24,384]{2,1,0:T(8,128)(2,1)} %get-tuple-element.9), calls=%async_computation | async-start | bytes 4718592 | tf_op jit(solution)/shard_map/all_to_all | solution.py:441
  145.5 0.0 copy-done.1
  145.5 0.1 copy.24
  145.6 0.2 fusion.9
  145.8 0.1 fusion.10
  146.0 0.4 select_reduce_fusion
  146.4 0.1 copy.26
  146.5 0.1 eq.18
  146.6 0.0 copy-done
  146.6 4.0 %fusion.2 = bf16[1536,768]{1,0:T(8,128)(2,1)} fusion(s32[1024]{0:T(1024)S(1)} %eq.18, bf16[128,8,768]{2,1,0:T(8,128)(2,1)S(1)} %copy-done), kind=kOutput, calls=%fused_computation.4 | convolution fusion | flops 2418671616 | bytes 3936256 | tf_op jit(solution)/shard_map/dot_general | solution.py:436
  150.6 5.8 %reshape.38 = bf16[128,12,2,384]{3,2,1,0:T(2,128)(2,1)} reshape(bf16[1536,768]{1,0:T(8,128)(2,1)} %fusion.2) | data formatting | bytes 4718592 | tf_op jit(solution)/shard_map/reshape | solution.py:444
  156.4 2.1 copy.29
  158.5 2.8 %copy.30 = bf16[128,24,384]{2,1,0:T(8,128)(2,1)} copy(bf16[128,24,384]{2,0,1:T(8,128)(2,1)S(1)} %bitcast.29) | data formatting | bytes 4718592 | tf_op jit(solution)/shard_map/reshape | solution.py:444
  161.3 17.3 %all-to-all-done = bf16[128,24,384]{2,1,0:T(8,128)(2,1)} async-done(((bf16[128,24,384]{2,1,0:T(8,128)(2,1)}), bf16[128,24,384]{2,1,0:T(8,128)(2,1)}, u32[]{:S(2)}, u32[]{:S(2)}) %all-to-all-start) | async-done | bytes 2359328 | tf_op jit(solution)/shard_map/all_to_all | solution.py:441
  178.6 5.0 %all-to-all-start.1 = ((bf16[128,24,384]{2,1,0:T(8,128)(2,1)}), bf16[128,24,384]{2,1,0:T(8,128)(2,1)}, u32[]{:S(2)}, u32[]{:S(2)}) async-start(bf16[128,24,384]{2,1,0:T(8,128)(2,1)} %copy.30), calls=%async_computation.1 | async-start | bytes 4718592 | tf_op jit(solution)/shard_map/all_to_all | solution.py:441
  183.6 2.1 copy.27
  185.6 2.4 %copy.28 = bf16[128,12,2,384]{3,2,1,0:T(2,128)(2,1)S(1)} copy(bf16[128,12,2,384]{3,0,1,2:T(8,128)(2,1)S(1)} %bitcast.30) | data formatting | bytes 4718592 | tf_op jit(solution)/shard_map/transpose | solution.py:457
  188.1 0.5 copy.31
  188.6 4.2 %fusion.7 = bf16[128,8,768]{2,1,0:T(8,128)(2,1)} fusion(bf16[1536,768]{1,0:T(8,128)(2,1)S(1)} %bitcast.32, s32[1024]{0:T(1024)S(1)} %eq.18), kind=kOutput, calls=%fused_computation.12 | convolution fusion | flops 2418278400 | bytes 3936256 | tf_op jit(solution)/shard_map/dot_general | solution.py:458
  192.8 24.0 %all-to-all-done.1.got_ref = bf16[128,24,384]{2,1,0:T(8,128)(2,1)} async-done(((bf16[128,24,384]{2,1,0:T(8,128)(2,1)}), bf16[128,24,384]{2,1,0:T(8,128)(2,1)}, u32[]{:S(2)}, u32[]{:S(2)}) %all-to-all-start.1) | async-done | bytes 2359328 | tf_op jit(solution)/shard_map/all_to_all | solution.py:441
  216.8 5.3 %shard_map.87 = (bf16[1536,768]{1,0:T(8,128)(2,1)S(1)}, bf16[1536,768]{1,0:T(8,128)(2,1)S(1)}, bf16[1536,768]{1,0:T(8,128)(2,1)S(1)}) custom-call(bf16[128,24,384]{2,1,0:T(8,128)(2,1)} %all-to-all-done.1.got_ref), custom_call_target="tpu_custom_call" | custom-call | bytes 10485760 | tf_op jit(solution)/shard_map/pallas_call | solution.py:405
  222.1 0.0 copy-start.3
  222.1 6.8 %convolution_convert_fusion = bf16[768,1536]{1,0:T(8,128)(2,1)S(1)} fusion(bf16[1536,768]{1,0:T(8,128)(2,1)S(1)} %get-tuple-element.14, bf16[1536,1536]{1,0:T(8,128)(2,1)} %bitcast.35), kind=kOutput, calls=%fused_computation.5 | convolution fusion | flops 3625058304 | bytes 9437184 | tf_op jit(solution)/shard_map/dot_general | solution.py:448
  229.0 0.0 copy-done.3
  229.0 0.0 copy-start.2
  229.0 3.3 %convolution_convert_fusion.1 = bf16[768,1280]{1,0:T(8,128)(2,1)S(1)} fusion(bf16[1536,768]{1,0:T(8,128)(2,1)S(1)} %get-tuple-element.12, bf16[1536,1280]{1,0:T(8,128)(2,1)S(1)} %bitcast.37), kind=kOutput, calls=%fused_computation.6 | convolution fusion | flops 3020881920 | bytes 8257536 | tf_op jit(solution)/shard_map/dot_general | solution.py:448
  232.3 0.0 copy-done.2
  232.3 3.3 %convolution_convert_fusion.2 = bf16[768,1280]{1,0:T(8,128)(2,1)S(1)} fusion(bf16[1536,768]{1,0:T(8,128)(2,1)S(1)} %get-tuple-element.10, bf16[1536,1280]{1,0:T(8,128)(2,1)S(1)} %bitcast.36), kind=kOutput, calls=%fused_computation.7 | convolution fusion | flops 3020881920 | bytes 8257536 | tf_op jit(solution)/shard_map/dot_general | solution.py:448
  235.6 3.2 %maximum_bitcast_fusion = bf16[1,768,4096]{2,1,0:T(8,128)(2,1)} fusion(bf16[768,1536]{1,0:T(8,128)(2,1)S(1)} %convolution_convert_fusion, bf16[768,1280]{1,0:T(8,128)(2,1)S(1)} %convolution_convert_fusion.1, bf16[768,1280]{1,0:T(8,128)(2,1)S(1)} %convolution_convert_fusion.2), kind=kLoop, calls=%fused_computation | loop fusion | flops 18874368 | bytes 12582912 | tf_op jit(solution)/shard_map/broadcast_in_dim | solution.py:461
  (2 shorter events, 0.1 us)
Async XLA Ops:
  0.6 146.0 %copy-start = (bf16[128,8,768]{2,1,0:T(8,128)(2,1)S(1)}, bf16[128,8,768]{2,1,0:T(8,128)(2,1)}, u32[]{:S(2)}) copy-start(bf16[128,8,768]{2,1,0:T(8,128)(2,1)} %param.7) | copy-start | bytes 4718596
  140.4 5.0 %copy-start.1 = (s32[128,8]{0,1:T(8,128)S(1)}, s32[128,8]{0,1:T(8,128)}, u32[]{:S(2)}) copy-start(s32[128,8]{0,1:T(8,128)} %param.9) | copy-start | bytes 12292
  140.5 38.1 %all-to-all-start = ((bf16[128,24,384]{2,1,0:T(8,128)(2,1)}), bf16[128,24,384]{2,1,0:T(8,128)(2,1)}, u32[]{:S(2)}, u32[]{:S(2)}) async-start(bf16[128,24,384]{2,1,0:T(8,128)(2,1)} %get-tuple-element.9), calls=%async_computation | async-start | bytes 4718592 | tf_op jit(solution)/shard_map/all_to_all | solution.py:441
  178.6 38.2 %all-to-all-start.1 = ((bf16[128,24,384]{2,1,0:T(8,128)(2,1)}), bf16[128,24,384]{2,1,0:T(8,128)(2,1)}, u32[]{:S(2)}, u32[]{:S(2)}) async-start(bf16[128,24,384]{2,1,0:T(8,128)(2,1)} %copy.30), calls=%async_computation.1 | async-start | bytes 4718592 | tf_op jit(solution)/shard_map/all_to_all | solution.py:441
  222.1 6.9 %copy-start.3 = (bf16[8,4,48,1280]{3,2,1,0:T(8,128)(2,1)S(1)}, bf16[8,4,48,1280]{3,2,1,0:T(8,128)(2,1)}, u32[]{:S(2)}) copy-start(bf16[8,4,48,1280]{3,2,1,0:T(8,128)(2,1)} %get-tuple-element.13) | copy-start | bytes 11796484
  229.0 3.3 %copy-start.2 = (bf16[8,4,48,1280]{3,2,1,0:T(8,128)(2,1)S(1)}, bf16[8,4,48,1280]{3,2,1,0:T(8,128)(2,1)}, u32[]{:S(2)}) copy-start(bf16[8,4,48,1280]{3,2,1,0:T(8,128)(2,1)} %get-tuple-element.11) | copy-start | bytes 11796484

commit v3 on v2

--- a/solution.py
+++ b/solution.py
@@ -10,6 +10,7 @@
 MESH = pl.DeviceIdType.MESH
 SIDE = 4
 CAP = 12
+STRIDE = 77
 PICK = SIDE * CAP
 WIDTHS = (1280, 1280, 1536)
 STARTS = (0, 1280, 2560)
@@ -51,11 +52,14 @@
     rollout_ref,
     adv_ref,
     grad_ref,
+    spot_ref,
+    hidden_ref,
     weight_ref,
     kept0,
     kept1,
     kept2,
     answer_ref,
+    got_hidden,
     weight,
     total,
     answer,
@@ -84,6 +88,8 @@
     mid_recv,
     last_send,
     last_recv,
+    hidden_send,
+    hidden_recv,
 ):
     outs, lines = (out0, out1, out2), (lines0, lines1, lines2)
     kept = (kept0, kept1, kept2)
@@ -91,17 +97,20 @@
     here, core = position()
 
     barrier = pltpu.get_barrier_semaphore()
-    for axis in range(3):
-        for by in range(SIDE):
-            for flip in range(2):
-                if (by or flip) and (by or axis == 0):
-                    pl.semaphore_signal(
-                        barrier,
-                        inc=1,
-                        device_id=place(moved(here, axis, by), (core + flip) % 2),
-                        device_id_type=MESH,
-                    )
-    pl.semaphore_wait(barrier, 19)
+    me = lax.axis_index("grp") * 32 + lax.axis_index("ep")
+
+    def other(index):
+        shift = (index * STRIDE) % 128
+        x, y, z = here
+        coords = ((x + shift // 2) % SIDE, (y + shift // 8) % SIDE, (z + shift // 32) % SIDE)
+        return place(coords, (core + shift) % 2)
+
+    def greet(index, carry):
+        pl.semaphore_signal(barrier, inc=1, device_id=other(index), device_id_type=MESH)
+        return carry
+
+    lax.fori_loop(1, 128, greet, 0)
+    pl.semaphore_wait(barrier, 127)
 
     def line_copy(part, by):
         there = place(moved(here, part, by), core)
@@ -175,6 +184,32 @@
             table_copy(part, by).start()
     for part in range(3):
         own_table(part).start()
+
+    def hidden_copy(index):
+        group, owner = other(index)
+        return pltpu.make_async_remote_copy(
+            src_ref=answer.at[group * 32 + owner],
+            dst_ref=got_hidden.at[me],
+            send_sem=hidden_send.at[index],
+            recv_sem=hidden_recv.at[index],
+            device_id=(group, owner),
+            device_id_type=MESH,
+        )
+
+    own_hidden = pltpu.make_async_copy(answer.at[me], got_hidden.at[me], local_sem.at[8])
+
+    def gather(block, carry):
+        wanted_spot = lax.broadcasted_iota(jnp.int32, (384, 1024), 0) + block * 384
+        pick = jnp.where(wanted_spot == spot_ref[...], 1.0, 0.0).astype(jnp.bfloat16)
+        found = jnp.dot(pick, hidden_ref[...], preferred_element_type=jnp.float32)
+        for i in range(32):
+            rows = found[i * CAP : i * CAP + CAP]
+            rows = jnp.concatenate([rows[:, :384], rows[:, 384:]], axis=0)
+            answer[block * 32 + i] = rows.astype(jnp.bfloat16)
+        return carry
+
+    lax.fori_loop(0, 4, gather, 0)
+    own_hidden.start()
 
     def mid_copy(part, by):
         return pltpu.make_async_remote_copy(
@@ -306,6 +341,10 @@
     total[...] = jnp.zeros_like(total)
     load_weight.wait()
 
+    def push(index, carry):
+        hidden_copy(index).start()
+        return carry
+
     def onward(step, carry):
         @pl.when(step < SIDE)
         def _():
@@ -313,11 +352,26 @@
                 mid_copy(part, step).wait()
                 forward(part, step, mids[part].at[step - 1])
 
+        @pl.when(step < SIDE - 1)
+        def _():
+            lax.fori_loop(64 * step - 63, jnp.minimum(64 * step + 1, 128), push, 0)
+
         for part in range(3):
             absorb(part, step - 1)
         return carry
 
     lax.fori_loop(1, SIDE + 1, onward, 0)
+
+    def settle(index, carry):
+        hidden_copy(index).wait_send()
+        return carry
+
+    def collect(index, carry):
+        hidden_copy(index).wait_recv()
+        return carry
+
+    own_hidden.wait()
+    lax.fori_loop(1, 128, settle, 0)
 
     def pack(device, carry):
         rows = total[device]
@@ -341,10 +395,11 @@
             return lax.fori_loop(1, 8, body, carry)
 
         lax.fori_loop(0, SIDE, finish, 0)
+    lax.fori_loop(1, 128, collect, 0)
     give.wait()
 
 
-def dispatch(route_t, gate_t, rollout_ids, advantages, out_grad, down_weight):
+def dispatch(*operands):
     vmem = pl.BlockSpec(memory_space=pltpu.VMEM)
     hbm = pl.BlockSpec(memory_space=pl.ANY)
     scratch = [
@@ -361,21 +416,22 @@
     ]
     scratch += [pltpu.VMEM((SIDE, 8 * PICK, w), jnp.bfloat16) for w in WIDTHS]
     scratch += [pltpu.VMEM((SIDE - 1, 8 * PICK, w), jnp.bfloat16) for w in WIDTHS]
-    scratch += [pltpu.SemaphoreType.DMA((8,))]
+    scratch += [pltpu.SemaphoreType.DMA((9,))]
     scratch += [pltpu.SemaphoreType.DMA((3, SIDE)) for _ in range(7)]
     scratch += [pltpu.SemaphoreType.DMA((3, SIDE, 8)) for _ in range(2)]
+    scratch += [pltpu.SemaphoreType.DMA((128,)) for _ in range(2)]
     shapes = [jax.ShapeDtypeStruct((8, SIDE, PICK, w), jnp.bfloat16) for w in WIDTHS]
-    shapes += [jax.ShapeDtypeStruct((128, 2 * CAP, 384), jnp.bfloat16)]
+    shapes += [jax.ShapeDtypeStruct((128, 2 * CAP, 384), jnp.bfloat16)] * 2
     return pl.pallas_call(
         dispatch_kernel,
         out_shape=shapes,
-        in_specs=[vmem] * 5 + [hbm],
-        out_specs=[hbm] * 4,
+        in_specs=[vmem] * 7 + [hbm],
+        out_specs=[hbm] * 5,
         scratch_shapes=scratch,
         compiler_params=pltpu.CompilerParams(
             collective_id=0, has_side_effects=True, vmem_limit_bytes=62 << 20
         ),
-    )(route_t, gate_t, rollout_ids, advantages, out_grad, down_weight)
+    )(*operands)
 
 
 def arrange_kernel(got_ref, *out_refs):
@@ -431,18 +487,20 @@
     one_hot = (jnp.arange(1536, dtype=jnp.int32)[:, None] == spot[None, :]).astype(jnp.bfloat16)
 
     parts = dispatch(
-        route_ids.T, gate_vals.T, rollout_ids, advantages, out_grad, down_weight
+        route_ids.T,
+        gate_vals.T,
+        rollout_ids,
+        advantages,
+        out_grad,
+        spot[None, :],
+        hidden.reshape(slots, 768),
+        down_weight,
     )
-    hidden_send = jnp.dot(
-        one_hot, hidden.reshape(slots, 768), preferred_element_type=jnp.float32
-    ).astype(jnp.bfloat16)
 
     def exchange(rows):
         return lax.all_to_all(rows, ("grp", "ep"), split_axis=0, concat_axis=0, tiled=True)
 
-    got_hidden = exchange(
-        hidden_send.reshape(128, CAP, 2, 384).transpose(0, 2, 1, 3).reshape(128, 2 * CAP, 384)
-    )
+    got_hidden = parts[4]
     returned = exchange(parts[3])
     grads = [
         lax.dot_general(

time: 239 us -> 227 us (0.950)
  waiting for transfers between devices: 41.3 us -> 4.41 us
  Pallas kernels: 145 us -> 178 us
  local copies, waits for them, and re-layouts: 16 us -> 9.54 us
  starting transfers between devices: 9.98 us -> 6.62 us
    all_to_all x2 -> x1, waiting for transfers between devices: 41.3 us -> 4.41 us  [exchange(): lax.all_to_all(rows, ('grp', 'ep'), split_axis=0, concat_axis=0, tiled=True)]
    pallas_call x1, Pallas kernels: 140 us -> 174 us  [dispatch(): pl.pallas_call(dispatch_kernel, out_shape=shapes, in_specs=[vmem] * 7 + [...]
    reshape x3 -> x0, local copies, waits for them, and re-layouts: 10.6 us -> none  [shards(): hidden_send.reshape(128, CAP, 2, 384).transpose(0, 2, 1, 3)]
    dot_general x3, matrix products: 13.4 us -> 18.8 us  [shards(): lax.dot_general(rows, part.reshape(1536, width), (((0,), (0,)), ((), ()))...]
    dot_general x1 -> x0, matrix products: 4.02 us -> none  [shards(): jnp.dot(one_hot, hidden.reshape(slots, 768), preferred_element_type=jnp.f...]
    unnamed x10 -> x14, local copies, waits for them, and re-layouts: 0.61 us -> 4.11 us
    all_to_all x2 -> x1, starting transfers between devices: 9.98 us -> 6.62 us  [exchange(): lax.all_to_all(rows, ('grp', 'ep'), split_axis=0, concat_axis=0, tiled=True)]
  transfers between devices with their start and end apart: 2 -> 1, of which waited for: 2 -> 1; matrix products, arithmetic and copies ran while one was open for 10% -> 10% of each run, Pallas kernels for 0% -> 2%
where the time goes in v3:
time: 227 us
  Pallas kernels  178 us (78%)
  matrix products  23.2 us (10%)
  local copies, waits for them, and re-layouts  9.54 us (4%)
  starting transfers between devices  6.62 us (3%)
  other arithmetic  4.52 us (2%)
  waiting for transfers between devices  4.41 us (2%)
    pallas_call x1, Pallas kernels, dispatch(): pl.pallas_call(dispatch_kernel, out_shape=shapes, in_specs=[vmem] * 7 + [...  174 us
    dot_general x3, matrix products, shards(): lax.dot_general(rows, part.reshape(1536, width), (((0,), (0,)), ((), ()))...  18.8 us
    all_to_all x1, starting transfers between devices, exchange(): lax.all_to_all(rows, ('grp', 'ep'), split_axis=0, concat_axis=0, tiled=True)  6.62 us
  transfers between devices with their start and end apart: 1, of which 1 were waited for; matrix products, arithmetic and copies ran while one was open for 10% of the time, Pallas kernels for 2%

profile of v3, /device:TPU:1, one launch (start us, length us, event | category | flops | bytes accessed | tf_op | source)
XLA Modules:
  0.0 226.9 jit_solution(3624555591084616776)
XLA Ops:
  0.6 0.8 copy.21
  1.4 0.2 fusion.5
  1.7 0.1 fusion.6
  1.8 0.4 select_reduce_fusion
  2.2 0.7 convert_add_fusion
  2.9 0.1 copy.23
  3.0 0.7 broadcast_in_dim_reshape.4.spot_ref
  3.7 174.1 %shard_map.86 = (bf16[8,4,48,1280]{3,2,1,0:T(8,128)(2,1)}, bf16[8,4,48,1280]{3,2,1,0:T(8,128)(2,1)}, bf16[8,4,48,1536]{3,2,1,0:T(8,128)(2,1)}, bf16[128,24,384]{2,1,0:T(8,128)(2,1)}, bf16[128,24,384]{2,1,0:T(8,128)(2,1)}) custom-call(s32[8,128]{1,0:T(8,128)} %bitcast.28, f32[8,128]{1,0:T(8,128)} %bitcast.29, s32[1,128]{1,0:T(1,128)} %rollout_ref.1, ...), custom_call_target="tpu_custom_call" | custom-call | tf_op jit(solution)/shard_map/pallas_call | solution.py:425
  177.9 0.0 copy-start
  177.9 6.6 %all-to-all-start = ((bf16[128,24,384]{2,1,0:T(8,128)(2,1)}), bf16[128,24,384]{2,1,0:T(8,128)(2,1)}, u32[]{:S(2)}, u32[]{:S(2)}) async-start(bf16[128,24,384]{2,1,0:T(8,128)(2,1)} %get-tuple-element.10), calls=%async_computation | async-start | bytes 4718592 | tf_op jit(solution)/shard_map/all_to_all | solution.py:501
  184.5 0.0 copy-done
  184.5 3.7 %shard_map.87 = (bf16[1536,768]{1,0:T(8,128)(2,1)S(1)}, bf16[1536,768]{1,0:T(8,128)(2,1)S(1)}, bf16[1536,768]{1,0:T(8,128)(2,1)S(1)}) custom-call(bf16[128,24,384]{2,1,0:T(8,128)(2,1)S(1)} %copy-done), custom_call_target="tpu_custom_call" | custom-call | bytes 10485760 | tf_op jit(solution)/shard_map/pallas_call | solution.py:461
  188.2 0.0 copy-start.1
  188.2 1.4 copy-done.1
  189.6 0.0 copy-start.3
  189.6 1.4 copy-done.3
  191.0 0.0 copy-start.4
  191.0 6.7 %convolution_convert_fusion.2 = bf16[768,1280]{1,0:T(8,128)(2,1)} fusion(bf16[1536,768]{1,0:T(8,128)(2,1)S(1)} %get-tuple-element.12, bf16[1536,1280]{1,0:T(8,128)(2,1)} %bitcast.32), kind=kOutput, calls=%fused_computation.5 | convolution fusion | flops 3020881920 | bytes 8257536 | tf_op jit(solution)/shard_map/dot_general | solution.py:506
  197.7 0.1 eq.18
  197.8 0.0 copy-done.4
  197.8 0.0 copy-start.2
  197.9 5.5 %convolution_convert_fusion.1 = bf16[768,1280]{1,0:T(8,128)(2,1)S(1)} fusion(bf16[1536,768]{1,0:T(8,128)(2,1)S(1)} %copy-done.4, bf16[1536,1280]{1,0:T(8,128)(2,1)} %bitcast.31), kind=kOutput, calls=%fused_computation.4 | convolution fusion | flops 3020881920 | bytes 8257536 | tf_op jit(solution)/shard_map/dot_general | solution.py:506
  203.4 0.0 copy-done.2
  203.4 0.0 copy-start.5
  203.4 6.6 %convolution_convert_fusion = bf16[768,1536]{1,0:T(8,128)(2,1)S(1)} fusion(bf16[1536,768]{1,0:T(8,128)(2,1)S(1)} %copy-done.2, bf16[1536,1536]{1,0:T(8,128)(2,1)} %bitcast.30), kind=kOutput, calls=%fused_computation.3 | convolution fusion | flops 3625058304 | bytes 9437184 | tf_op jit(solution)/shard_map/dot_general | solution.py:506
  210.0 0.0 copy-done.5
  210.0 3.2 %maximum_bitcast_fusion = bf16[1,768,4096]{2,1,0:T(8,128)(2,1)} fusion(bf16[768,1536]{1,0:T(8,128)(2,1)S(1)} %convolution_convert_fusion, bf16[768,1280]{1,0:T(8,128)(2,1)S(1)} %convolution_convert_fusion.1, bf16[768,1280]{1,0:T(8,128)(2,1)S(1)} %copy-done.5), kind=kLoop, calls=%fused_computation | loop fusion | flops 18874368 | bytes 12582912 | tf_op jit(solution)/shard_map/broadcast_in_dim | solution.py:519
  213.2 4.4 %all-to-all-done = bf16[128,24,384]{2,1,0:T(8,128)(2,1)} async-done(((bf16[128,24,384]{2,1,0:T(8,128)(2,1)}), bf16[128,24,384]{2,1,0:T(8,128)(2,1)}, u32[]{:S(2)}, u32[]{:S(2)}) %all-to-all-start) | async-done | bytes 2359328 | tf_op jit(solution)/shard_map/all_to_all | solution.py:501
  217.6 2.1 copy.25
  219.7 2.4 %copy.26 = bf16[128,12,2,384]{3,2,1,0:T(2,128)(2,1)S(1)} copy(bf16[128,12,2,384]{3,0,1,2:T(8,128)(2,1)S(1)} %bitcast.24) | data formatting | bytes 4718592 | tf_op jit(solution)/shard_map/transpose | solution.py:515
  222.1 0.5 copy.27
  222.6 4.2 %fusion.3 = bf16[128,8,768]{2,1,0:T(8,128)(2,1)} fusion(bf16[1536,768]{1,0:T(8,128)(2,1)S(1)} %bitcast.26, s32[1024]{0:T(1024)S(1)} %eq.18), kind=kOutput, calls=%fused_computation.8 | convolution fusion | flops 2418278400 | bytes 3936256 | tf_op jit(solution)/shard_map/dot_general | solution.py:516
  (1 shorter events, 0.0 us)
Async XLA Ops:
  177.9 6.6 %copy-start = (bf16[128,24,384]{2,1,0:T(8,128)(2,1)S(1)}, bf16[128,24,384]{2,1,0:T(8,128)(2,1)}, u32[]{:S(2)}) copy-start(bf16[128,24,384]{2,1,0:T(8,128)(2,1)} %get-tuple-element.11.got_ref) | copy-start | bytes 7077892
  177.9 39.7 %all-to-all-start = ((bf16[128,24,384]{2,1,0:T(8,128)(2,1)}), bf16[128,24,384]{2,1,0:T(8,128)(2,1)}, u32[]{:S(2)}, u32[]{:S(2)}) async-start(bf16[128,24,384]{2,1,0:T(8,128)(2,1)} %get-tuple-element.10), calls=%async_computation | async-start | bytes 4718592 | tf_op jit(solution)/shard_map/all_to_all | solution.py:501
  188.2 1.4 copy-start.1
  189.6 1.4 copy-start.3
  191.0 6.8 %copy-start.4 = (bf16[1536,768]{1,0:T(8,128)(2,1)S(1)}, bf16[1536,768]{1,0:T(8,128)(2,1)}, u32[]{:S(2)}) copy-start(bf16[1536,768]{1,0:T(8,128)(2,1)} %copy-done.3) | copy-start | bytes 7077892
  197.8 5.6 %copy-start.2 = (bf16[1536,768]{1,0:T(8,128)(2,1)S(1)}, bf16[1536,768]{1,0:T(8,128)(2,1)}, u32[]{:S(2)}) copy-start(bf16[1536,768]{1,0:T(8,128)(2,1)} %copy-done.1) | copy-start | bytes 7077892
  203.4 6.6 %copy-start.5 = (bf16[768,1280]{1,0:T(8,128)(2,1)S(1)}, bf16[768,1280]{1,0:T(8,128)(2,1)}, u32[]{:S(2)}) copy-start(bf16[768,1280]{1,0:T(8,128)(2,1)} %convolution_convert_fusion.2) | copy-start | bytes 5898244

commit v4 on v3

--- a/solution.py
+++ b/solution.py
@@ -1,5 +1,3 @@
-import functools
-
 import jax
 import jax.numpy as jnp
 from jax import lax
@@ -470,7 +468,6 @@
 
 def shards(hidden, out_grad, route_ids, gate_vals, rollout_ids, advantages, down_weight):
     slots = 1024
-    flat_ids = route_ids.reshape(slots)
     named = jnp.sum(
         (route_ids[:, :, None] == jnp.arange(128, dtype=jnp.int32)).astype(jnp.bfloat16), axis=1
     )

time: 227 us -> 227 us (level)
  no operation moved by 1% of the time
where the time goes in v4:
time: 227 us
  Pallas kernels  178 us (78%)
  matrix products  23.2 us (10%)
  local copies, waits for them, and re-layouts  9.54 us (4%)
  starting transfers between devices  6.62 us (3%)
  other arithmetic  4.52 us (2%)
  waiting for transfers between devices  4.41 us (2%)
    pallas_call x1, Pallas kernels, dispatch(): pl.pallas_call(dispatch_kernel, out_shape=shapes, in_specs=[vmem] * 7 + [...  174 us
    dot_general x3, matrix products, shards(): lax.dot_general(rows, part.reshape(1536, width), (((0,), (0,)), ((), ()))...  18.8 us
    all_to_all x1, starting transfers between devices, exchange(): lax.all_to_all(rows, ('grp', 'ep'), split_axis=0, concat_axis=0, tiled=True)  6.62 us
  transfers between devices with their start and end apart: 1, of which 1 were waited for; matrix products, arithmetic and copies ran while one was open for 10% of the time, Pallas kernels for 2%

profile of v4, /device:TPU:1, one launch (start us, length us, event | category | flops | bytes accessed | tf_op | source)
XLA Modules:
  0.0 226.9 jit_solution(3624555591084616776)
XLA Ops:
  0.6 0.8 copy.21
  1.4 0.2 fusion.5
  1.7 0.1 fusion.6
  1.8 0.4 select_reduce_fusion
  2.2 0.7 convert_add_fusion
  2.9 0.1 copy.23
  3.0 0.7 broadcast_in_dim_reshape.4.spot_ref
  3.7 174.1 %shard_map.86 = (bf16[8,4,48,1280]{3,2,1,0:T(8,128)(2,1)}, bf16[8,4,48,1280]{3,2,1,0:T(8,128)(2,1)}, bf16[8,4,48,1536]{3,2,1,0:T(8,128)(2,1)}, bf16[128,24,384]{2,1,0:T(8,128)(2,1)}, bf16[128,24,384]{2,1,0:T(8,128)(2,1)}) custom-call(s32[8,128]{1,0:T(8,128)} %bitcast.28, f32[8,128]{1,0:T(8,128)} %bitcast.29, s32[1,128]{1,0:T(1,128)} %rollout_ref.1, ...), custom_call_target="tpu_custom_call" | custom-call | tf_op jit(solution)/shard_map/pallas_call | solution.py:423
  177.9 0.0 copy-start
  177.9 6.6 %all-to-all-start = ((bf16[128,24,384]{2,1,0:T(8,128)(2,1)}), bf16[128,24,384]{2,1,0:T(8,128)(2,1)}, u32[]{:S(2)}, u32[]{:S(2)}) async-start(bf16[128,24,384]{2,1,0:T(8,128)(2,1)} %get-tuple-element.10), calls=%async_computation | async-start | bytes 4718592 | tf_op jit(solution)/shard_map/all_to_all | solution.py:498
  184.5 0.0 copy-done
  184.5 3.7 %shard_map.87 = (bf16[1536,768]{1,0:T(8,128)(2,1)S(1)}, bf16[1536,768]{1,0:T(8,128)(2,1)S(1)}, bf16[1536,768]{1,0:T(8,128)(2,1)S(1)}) custom-call(bf16[128,24,384]{2,1,0:T(8,128)(2,1)S(1)} %copy-done), custom_call_target="tpu_custom_call" | custom-call | bytes 10485760 | tf_op jit(solution)/shard_map/pallas_call | solution.py:459
  188.2 0.0 copy-start.1
  188.2 1.4 copy-done.1
  189.6 0.0 copy-start.3
  189.6 1.4 copy-done.3
  191.0 0.0 copy-start.4
  191.0 6.7 %convolution_convert_fusion.2 = bf16[768,1280]{1,0:T(8,128)(2,1)} fusion(bf16[1536,768]{1,0:T(8,128)(2,1)S(1)} %get-tuple-element.12, bf16[1536,1280]{1,0:T(8,128)(2,1)} %bitcast.32), kind=kOutput, calls=%fused_computation.5 | convolution fusion | flops 3020881920 | bytes 8257536 | tf_op jit(solution)/shard_map/dot_general | solution.py:503
  197.7 0.1 eq.18
  197.8 0.0 copy-done.4
  197.8 0.0 copy-start.2
  197.9 5.5 %convolution_convert_fusion.1 = bf16[768,1280]{1,0:T(8,128)(2,1)S(1)} fusion(bf16[1536,768]{1,0:T(8,128)(2,1)S(1)} %copy-done.4, bf16[1536,1280]{1,0:T(8,128)(2,1)} %bitcast.31), kind=kOutput, calls=%fused_computation.4 | convolution fusion | flops 3020881920 | bytes 8257536 | tf_op jit(solution)/shard_map/dot_general | solution.py:503
  203.4 0.0 copy-done.2
  203.4 0.0 copy-start.5
  203.4 6.6 %convolution_convert_fusion = bf16[768,1536]{1,0:T(8,128)(2,1)S(1)} fusion(bf16[1536,768]{1,0:T(8,128)(2,1)S(1)} %copy-done.2, bf16[1536,1536]{1,0:T(8,128)(2,1)} %bitcast.30), kind=kOutput, calls=%fused_computation.3 | convolution fusion | flops 3625058304 | bytes 9437184 | tf_op jit(solution)/shard_map/dot_general | solution.py:503
  210.0 0.0 copy-done.5
  210.0 3.2 %maximum_bitcast_fusion = bf16[1,768,4096]{2,1,0:T(8,128)(2,1)} fusion(bf16[768,1536]{1,0:T(8,128)(2,1)S(1)} %convolution_convert_fusion, bf16[768,1280]{1,0:T(8,128)(2,1)S(1)} %convolution_convert_fusion.1, bf16[768,1280]{1,0:T(8,128)(2,1)S(1)} %copy-done.5), kind=kLoop, calls=%fused_computation | loop fusion | flops 18874368 | bytes 12582912 | tf_op jit(solution)/shard_map/broadcast_in_dim | solution.py:516
  213.2 4.4 %all-to-all-done = bf16[128,24,384]{2,1,0:T(8,128)(2,1)} async-done(((bf16[128,24,384]{2,1,0:T(8,128)(2,1)}), bf16[128,24,384]{2,1,0:T(8,128)(2,1)}, u32[]{:S(2)}, u32[]{:S(2)}) %all-to-all-start) | async-done | bytes 2359328 | tf_op jit(solution)/shard_map/all_to_all | solution.py:498
  217.6 2.1 copy.25
  219.7 2.4 %copy.26 = bf16[128,12,2,384]{3,2,1,0:T(2,128)(2,1)S(1)} copy(bf16[128,12,2,384]{3,0,1,2:T(8,128)(2,1)S(1)} %bitcast.24) | data formatting | bytes 4718592 | tf_op jit(solution)/shard_map/transpose | solution.py:512
  222.1 0.5 copy.27
  222.6 4.2 %fusion.3 = bf16[128,8,768]{2,1,0:T(8,128)(2,1)} fusion(bf16[1536,768]{1,0:T(8,128)(2,1)S(1)} %bitcast.26, s32[1024]{0:T(1024)S(1)} %eq.18), kind=kOutput, calls=%fused_computation.8 | convolution fusion | flops 2418278400 | bytes 3936256 | tf_op jit(solution)/shard_map/dot_general | solution.py:513
  (1 shorter events, 0.0 us)
Async XLA Ops:
  177.9 6.6 %copy-start = (bf16[128,24,384]{2,1,0:T(8,128)(2,1)S(1)}, bf16[128,24,384]{2,1,0:T(8,128)(2,1)}, u32[]{:S(2)}) copy-start(bf16[128,24,384]{2,1,0:T(8,128)(2,1)} %get-tuple-element.11.got_ref) | copy-start | bytes 7077892
  177.9 39.7 %all-to-all-start = ((bf16[128,24,384]{2,1,0:T(8,128)(2,1)}), bf16[128,24,384]{2,1,0:T(8,128)(2,1)}, u32[]{:S(2)}, u32[]{:S(2)}) async-start(bf16[128,24,384]{2,1,0:T(8,128)(2,1)} %get-tuple-element.10), calls=%async_computation | async-start | bytes 4718592 | tf_op jit(solution)/shard_map/all_to_all | solution.py:498
  188.2 1.4 copy-start.1
  189.6 1.4 copy-start.3
  191.0 6.8 %copy-start.4 = (bf16[1536,768]{1,0:T(8,128)(2,1)S(1)}, bf16[1536,768]{1,0:T(8,128)(2,1)}, u32[]{:S(2)}) copy-start(bf16[1536,768]{1,0:T(8,128)(2,1)} %copy-done.3) | copy-start | bytes 7077892
  197.8 5.6 %copy-start.2 = (bf16[1536,768]{1,0:T(8,128)(2,1)S(1)}, bf16[1536,768]{1,0:T(8,128)(2,1)}, u32[]{:S(2)}) copy-start(bf16[1536,768]{1,0:T(8,128)(2,1)} %copy-done.1) | copy-start | bytes 7077892
  203.4 6.6 %copy-start.5 = (bf16[768,1280]{1,0:T(8,128)(2,1)S(1)}, bf16[768,1280]{1,0:T(8,128)(2,1)}, u32[]{:S(2)}) copy-start(bf16[768,1280]{1,0:T(8,128)(2,1)} %convolution_convert_fusion.2) | copy-start | bytes 5898244

commit v5 on v4

--- a/solution.py
+++ b/solution.py
@@ -98,10 +98,10 @@
     me = lax.axis_index("grp") * 32 + lax.axis_index("ep")
 
     def other(index):
-        shift = (index * STRIDE) % 128
+        shift = (index * STRIDE) & 127
         x, y, z = here
-        coords = ((x + shift // 2) % SIDE, (y + shift // 8) % SIDE, (z + shift // 32) % SIDE)
-        return place(coords, (core + shift) % 2)
+        x, y, z = (x + (shift >> 1)) & 3, (y + (shift >> 3)) & 3, (z + (shift >> 5)) & 3
+        return ((z & 2) + ((core + shift) & 1), y * 8 + x * 2 + (z & 1))
 
     def greet(index, carry):
         pl.semaphore_signal(barrier, inc=1, device_id=other(index), device_id_type=MESH)
@@ -466,6 +466,37 @@
     )(got)
 
 
+def restore_kernel(spot_ref, got_ref, out_ref, rows):
+    def stage(block, carry):
+        pieces = []
+        for j in range(SIDE):
+            piece = got_ref[block * SIDE + j].astype(jnp.float32)
+            pieces.append(jnp.concatenate([piece[:CAP], piece[CAP:]], axis=1))
+        first = pl.multiple_of(block * PICK, PICK)
+        rows[pl.ds(first, PICK)] = jnp.concatenate(pieces, axis=0).astype(jnp.bfloat16)
+        return carry
+
+    lax.fori_loop(0, 32, stage, 0)
+    for first in range(0, 1024, 256):
+        place_of = lax.broadcasted_iota(jnp.int32, (256, 1536), 1)
+        pick = jnp.where(spot_ref[first : first + 256] == place_of, 1.0, 0.0)
+        out_ref[first : first + 256] = jnp.dot(
+            pick.astype(jnp.bfloat16), rows[...], preferred_element_type=jnp.float32
+        ).astype(jnp.bfloat16)
+
+
+def restore(spot, got):
+    vmem = pl.BlockSpec(memory_space=pltpu.VMEM)
+    return pl.pallas_call(
+        restore_kernel,
+        out_shape=jax.ShapeDtypeStruct((1024, 768), jnp.bfloat16),
+        in_specs=[vmem] * 2,
+        out_specs=vmem,
+        scratch_shapes=[pltpu.VMEM((1536, 768), jnp.bfloat16)],
+        compiler_params=pltpu.CompilerParams(vmem_limit_bytes=24 << 20),
+    )(spot, got)
+
+
 def shards(hidden, out_grad, route_ids, gate_vals, rollout_ids, advantages, down_weight):
     slots = 1024
     named = jnp.sum(
@@ -481,7 +512,6 @@
         axis=2,
     ).astype(jnp.int32)
     spot = (route_ids * CAP + rank).reshape(slots)
-    one_hot = (jnp.arange(1536, dtype=jnp.int32)[:, None] == spot[None, :]).astype(jnp.bfloat16)
 
     parts = dispatch(
         route_ids.T,
@@ -509,10 +539,7 @@
         for rows, part, width in zip(arrange(got_hidden), parts[:3], WIDTHS)
     ]
     weight_grad = jnp.concatenate(grads, axis=1)
-    returned = returned.reshape(128, 2, CAP, 384).transpose(0, 2, 1, 3).reshape(1536, 768)
-    hidden_grad = lax.dot_general(
-        one_hot, returned, (((0,), (0,)), ((), ())), preferred_element_type=jnp.float32
-    ).astype(jnp.bfloat16)
+    hidden_grad = restore(spot[:, None], returned)
     return hidden_grad.reshape(128, 8, 768), weight_grad[None]
 
 

time: 227 us -> 219 us (0.965)
  matrix products: 23.2 us -> 19.5 us
  local copies, waits for them, and re-layouts: 9.54 us -> 6.26 us
    pallas_call x0 -> x1, Pallas kernels: none -> 4.46 us  [restore(): pl.pallas_call(restore_kernel, out_shape=jax.ShapeDtypeStruct((1024, 768)...]
    dot_general x1 -> x0, matrix products: 4.22 us -> none  [shards(): lax.dot_general(one_hot, returned, (((0,), (0,)), ((), ())), preferred_el...]
    pallas_call x1, Pallas kernels: 174 us -> 171 us  [dispatch(): pl.pallas_call(dispatch_kernel, out_shape=shapes, in_specs=[vmem] * 7 + [...]
    transpose x1 -> x0, local copies, waits for them, and re-layouts: 2.43 us -> none  [shards(): returned.reshape(128, 2, CAP, 384).transpose(0, 2, 1, 3).reshape(1536, 768)]
    unnamed x14 -> x11, local copies, waits for them, and re-layouts: 4.11 us -> 5.24 us
where the time goes in v5:
time: 219 us
  Pallas kernels  179 us (82%)
  matrix products  19.5 us (9%)
  local copies, waits for them, and re-layouts  6.26 us (3%)
  starting transfers between devices  5.8 us (3%)
  other arithmetic  4.52 us (2%)
  waiting for transfers between devices  2.49 us (1%)
    pallas_call x1, Pallas kernels, dispatch(): pl.pallas_call(dispatch_kernel, out_shape=shapes, in_specs=[vmem] * 7 + [...  171 us
    dot_general x3, matrix products, shards(): lax.dot_general(rows, part.reshape(1536, width), (((0,), (0,)), ((), ()))...  19.4 us
    all_to_all x1, starting transfers between devices, exchange(): lax.all_to_all(rows, ('grp', 'ep'), split_axis=0, concat_axis=0, tiled=True)  5.8 us
    unnamed x11, local copies, waits for them, and re-layouts  5.24 us
    pallas_call x1, Pallas kernels, restore(): pl.pallas_call(restore_kernel, out_shape=jax.ShapeDtypeStruct((1024, 768)...  4.46 us
  transfers between devices with their start and end apart: 1, of which 1 were waited for; matrix products, arithmetic and copies ran while one was open for 10% of the time, Pallas kernels for 2%

profile of v5, /device:TPU:1, one launch (start us, length us, event | category | flops | bytes accessed | tf_op | source)
XLA Modules:
  0.0 218.5 jit_solution(17927968121748795283)
XLA Ops:
  0.6 0.8 copy.20
  1.4 0.2 fusion.1
  1.7 0.1 fusion.2
  1.8 0.4 select_reduce_fusion
  2.2 0.7 convert_add_fusion
  2.9 0.1 copy.22
  3.0 0.7 broadcast_in_dim_reshape.7.spot_ref
  3.7 171.1 %shard_map.86 = (bf16[8,4,48,1280]{3,2,1,0:T(8,128)(2,1)}, bf16[8,4,48,1280]{3,2,1,0:T(8,128)(2,1)}, bf16[8,4,48,1536]{3,2,1,0:T(8,128)(2,1)}, bf16[128,24,384]{2,1,0:T(8,128)(2,1)}, bf16[128,24,384]{2,1,0:T(8,128)(2,1)}) custom-call(s32[8,128]{1,0:T(8,128)} %bitcast.18, f32[8,128]{1,0:T(8,128)} %bitcast.19, s32[1,128]{1,0:T(1,128)} %rollout_ref.1, ...), custom_call_target="tpu_custom_call" | custom-call | tf_op jit(solution)/shard_map/pallas_call | solution.py:423
  174.9 5.8 %all-to-all-start = ((bf16[128,24,384]{2,1,0:T(8,128)(2,1)}), bf16[128,24,384]{2,1,0:T(8,128)(2,1)S(1)}, u32[]{:S(2)}, u32[]{:S(2)}) async-start(bf16[128,24,384]{2,1,0:T(8,128)(2,1)} %get-tuple-element.10), calls=%async_computation | async-start | bytes 4718592 | tf_op jit(solution)/shard_map/all_to_all | solution.py:528
  180.7 0.0 copy-start
  180.7 1.7 copy-done
  182.3 3.6 %shard_map.88 = (bf16[1536,768]{1,0:T(8,128)(2,1)S(1)}, bf16[1536,768]{1,0:T(8,128)(2,1)S(1)}, bf16[1536,768]{1,0:T(8,128)(2,1)S(1)}) custom-call(bf16[128,24,384]{2,1,0:T(8,128)(2,1)S(1)} %copy-done), custom_call_target="tpu_custom_call" | custom-call | bytes 10485760 | tf_op jit(solution)/shard_map/pallas_call | solution.py:459
  186.0 0.0 copy-start.1
  186.0 1.4 copy-done.1
  187.4 0.0 copy-start.3
  187.4 1.4 copy-done.3
  188.8 6.5 %convolution_convert_fusion.2 = bf16[768,1280]{1,0:T(8,128)(2,1)} fusion(bf16[1536,768]{1,0:T(8,128)(2,1)S(1)} %get-tuple-element.12, bf16[1536,1280]{1,0:T(8,128)(2,1)} %bitcast.22), kind=kOutput, calls=%fused_computation.3 | convolution fusion | flops 3020881920 | bytes 8257536 | tf_op jit(solution)/shard_map/dot_general | solution.py:533
  195.3 0.2 broadcast_in_dim_reshape.8.spot_ref
  195.5 0.0 copy-start.2
  195.5 6.3 %convolution_convert_fusion.1 = bf16[768,1280]{1,0:T(8,128)(2,1)S(1)} fusion(bf16[1536,768]{1,0:T(8,128)(2,1)} %copy-done.3, bf16[1536,1280]{1,0:T(8,128)(2,1)} %bitcast.21), kind=kOutput, calls=%fused_computation.2 | convolution fusion | flops 3020881920 | bytes 8257536 | tf_op jit(solution)/shard_map/dot_general | solution.py:533
  201.8 0.0 copy-done.2
  201.8 0.0 copy-start.4
  201.8 6.6 %convolution_convert_fusion = bf16[768,1536]{1,0:T(8,128)(2,1)S(1)} fusion(bf16[1536,768]{1,0:T(8,128)(2,1)S(1)} %copy-done.2, bf16[1536,1536]{1,0:T(8,128)(2,1)} %bitcast.20), kind=kOutput, calls=%fused_computation.1 | convolution fusion | flops 3625058304 | bytes 9437184 | tf_op jit(solution)/shard_map/dot_general | solution.py:533
  208.4 0.0 copy-done.4
  208.4 3.2 %maximum_bitcast_fusion = bf16[1,768,4096]{2,1,0:T(8,128)(2,1)} fusion(bf16[768,1536]{1,0:T(8,128)(2,1)S(1)} %convolution_convert_fusion, bf16[768,1280]{1,0:T(8,128)(2,1)S(1)} %convolution_convert_fusion.1, bf16[768,1280]{1,0:T(8,128)(2,1)S(1)} %copy-done.4), kind=kLoop, calls=%fused_computation | loop fusion | flops 18874368 | bytes 12582912 | tf_op jit(solution)/shard_map/broadcast_in_dim | solution.py:543
  211.6 2.5 %all-to-all-done.got_ref = bf16[128,24,384]{2,1,0:T(8,128)(2,1)S(1)} async-done(((bf16[128,24,384]{2,1,0:T(8,128)(2,1)}), bf16[128,24,384]{2,1,0:T(8,128)(2,1)S(1)}, u32[]{:S(2)}, u32[]{:S(2)}) %all-to-all-start) | async-done | bytes 2359328 | tf_op jit(solution)/shard_map/all_to_all | solution.py:528
  214.1 4.5 %shard_map.87 = bf16[1024,768]{1,0:T(8,128)(2,1)} custom-call(s32[1024,1]{1,0:T(8,128)S(1)} %broadcast_in_dim_reshape.8.spot_ref, bf16[128,24,384]{2,1,0:T(8,128)(2,1)S(1)} %all-to-all-done.got_ref), custom_call_target="tpu_custom_call" | custom-call | tf_op jit(solution)/shard_map/pallas_call | solution.py:490
  (1 shorter events, 0.0 us)
Async XLA Ops:
  174.9 39.2 %all-to-all-start = ((bf16[128,24,384]{2,1,0:T(8,128)(2,1)}), bf16[128,24,384]{2,1,0:T(8,128)(2,1)S(1)}, u32[]{:S(2)}, u32[]{:S(2)}) async-start(bf16[128,24,384]{2,1,0:T(8,128)(2,1)} %get-tuple-element.10), calls=%async_computation | async-start | bytes 4718592 | tf_op jit(solution)/shard_map/all_to_all | solution.py:528
  180.7 1.7 copy-start
  186.0 1.4 copy-start.1
  187.4 1.4 copy-start.3
  195.5 6.3 %copy-start.2 = (bf16[1536,768]{1,0:T(8,128)(2,1)S(1)}, bf16[1536,768]{1,0:T(8,128)(2,1)}, u32[]{:S(2)}) copy-start(bf16[1536,768]{1,0:T(8,128)(2,1)} %copy-done.1) | copy-start | bytes 7077892
  201.8 6.6 %copy-start.4 = (bf16[768,1280]{1,0:T(8,128)(2,1)S(1)}, bf16[768,1280]{1,0:T(8,128)(2,1)}, u32[]{:S(2)}) copy-start(bf16[768,1280]{1,0:T(8,128)(2,1)} %convolution_convert_fusion.2) | copy-start | bytes 5898244

commit v6 on v5

--- a/solution.py
+++ b/solution.py
@@ -244,11 +244,13 @@
         src, dst, _, _ = last_copy(part, by, 0, 0, source)
         return pltpu.make_async_copy(src, dst, last_recv.at[part, by, 0])
 
-    def forward(part, by, source):
-        last_local(part, by, source).start()
+    def forward(by, sources):
+        for part in range(3):
+            last_local(part, by, sources[part]).start()
 
         def body(index, carry):
-            last_remote(part, by, index, source).start()
+            for part in range(3):
+                last_remote(part, by, (3 * index) & 7, sources[part]).start()
             return carry
 
         lax.fori_loop(1, 8, body, 0)
@@ -264,10 +266,9 @@
             line_copy(part, by).wait()
             table_copy(part, by).wait()
 
-    for part in range(3):
-
-        def select(i, carry, part=part):
-            by = (i + 1) % SIDE
+    def select(i, carry):
+        by = jnp.where(i < 2, 2 * i + 1, 6 - 2 * i)
+        for part in range(3):
             target = (here[(part + 1) % 3] + by) % SIDE
             first = pl.multiple_of(target * 8, 8)
             ranks = jnp.concatenate(
@@ -285,22 +286,21 @@
                 )
             factor = jnp.concatenate(scales, axis=0)
             for start in range(0, WIDTHS[part], 256):
-                width = min(256, WIDTHS[part] - start)
                 found = jnp.dot(
                     picks[...],
-                    lines[part][:, start : start + width],
+                    lines[part][:, start : start + 256],
                     preferred_element_type=jnp.float32,
                 )
-                sends[part][by, :, start : start + width] = (found * factor).astype(jnp.bfloat16)
+                sends[part][by, :, start : start + 256] = (found * factor).astype(jnp.bfloat16)
 
             @pl.when(by > 0)
             def _():
                 mid_copy(part, by).start()
 
-            return carry
-
-        lax.fori_loop(0, SIDE, select, 0)
-        forward(part, 0, sends[part].at[0])
+        return carry
+
+    lax.fori_loop(0, SIDE, select, 0)
+    forward(0, [sends[part].at[0] for part in range(3)])
 
     def keep(part, by):
         origin = (here[(part + 1) % 3] + SIDE - by) % SIDE
@@ -346,16 +346,17 @@
     def onward(step, carry):
         @pl.when(step < SIDE)
         def _():
+            turn = jnp.where(step < 3, 2 * step - 1, 2)
             for part in range(3):
-                mid_copy(part, step).wait()
-                forward(part, step, mids[part].at[step - 1])
-
-        @pl.when(step < SIDE - 1)
+                mid_copy(part, turn).wait()
+            forward(turn, [mids[part].at[turn - 1] for part in range(3)])
+
+        @pl.when(step < SIDE)
         def _():
-            lax.fori_loop(64 * step - 63, jnp.minimum(64 * step + 1, 128), push, 0)
+            lax.fori_loop(43 * step - 42, jnp.minimum(43 * step + 1, 128), push, 0)
 
         for part in range(3):
-            absorb(part, step - 1)
+            absorb(part, jnp.where(step < 2, 0, jnp.where(step < 4, 2 * step - 3, 2)))
         return carry
 
     lax.fori_loop(1, SIDE + 1, onward, 0)

time: 219 us -> 213 us (0.973)
  Pallas kernels: 179 us -> 171 us
  starting transfers between devices: 5.8 us -> 7.99 us
    pallas_call x1, Pallas kernels: 171 us -> 163 us  [dispatch(): pl.pallas_call(dispatch_kernel, out_shape=shapes, in_specs=[vmem] * 7 + [...]
    all_to_all x1, starting transfers between devices: 5.8 us -> 7.99 us  [exchange(): lax.all_to_all(rows, ('grp', 'ep'), split_axis=0, concat_axis=0, tiled=True)]
  transfers between devices with their start and end apart: 1 -> 1, of which waited for: 1 -> 1; matrix products, arithmetic and copies ran while one was open for 10% -> 11% of each run, Pallas kernels for 2% -> 2%
where the time goes in v6:
time: 213 us; the launch traced here: 212 us
  Pallas kernels  171 us (80%)
  matrix products  19.5 us (9%)
  starting transfers between devices  7.99 us (4%)
  local copies, waits for them, and re-layouts  6.26 us (3%)
  other arithmetic  4.52 us (2%)
  waiting for transfers between devices  2.49 us (1%)
    pallas_call x1, Pallas kernels, dispatch(): pl.pallas_call(dispatch_kernel, out_shape=shapes, in_specs=[vmem] * 7 + [...  163 us
    dot_general x3, matrix products, shards(): lax.dot_general(rows, part.reshape(1536, width), (((0,), (0,)), ((), ()))...  19.4 us
    all_to_all x1, starting transfers between devices, exchange(): lax.all_to_all(rows, ('grp', 'ep'), split_axis=0, concat_axis=0, tiled=True)  7.99 us
    unnamed x11, local copies, waits for them, and re-layouts  5.24 us
    pallas_call x1, Pallas kernels, restore(): pl.pallas_call(restore_kernel, out_shape=jax.ShapeDtypeStruct((1024, 768)...  4.46 us
  transfers between devices with their start and end apart: 1, of which 1 were waited for; matrix products, arithmetic and copies ran while one was open for 11% of the time, Pallas kernels for 2%

profile of v6, /device:TPU:1, one launch (start us, length us, event | category | flops | bytes accessed | tf_op | source)
XLA Modules:
  0.0 212.3 jit_solution(4099340217187981596)
XLA Ops:
  0.6 0.8 copy.20
  1.4 0.2 fusion.1
  1.7 0.1 fusion.2
  1.8 0.4 select_reduce_fusion
  2.2 0.7 convert_add_fusion
  2.9 0.1 copy.22
  3.0 0.7 broadcast_in_dim_reshape.7.spot_ref
  3.7 162.7 %shard_map.86 = (bf16[8,4,48,1280]{3,2,1,0:T(8,128)(2,1)}, bf16[8,4,48,1280]{3,2,1,0:T(8,128)(2,1)}, bf16[8,4,48,1536]{3,2,1,0:T(8,128)(2,1)}, bf16[128,24,384]{2,1,0:T(8,128)(2,1)}, bf16[128,24,384]{2,1,0:T(8,128)(2,1)}) custom-call(s32[8,128]{1,0:T(8,128)} %bitcast.18, f32[8,128]{1,0:T(8,128)} %bitcast.19, s32[1,128]{1,0:T(1,128)} %rollout_ref.1, ...), custom_call_target="tpu_custom_call" | custom-call | tf_op jit(solution)/shard_map/pallas_call | solution.py:424
  166.5 8.0 %all-to-all-start = ((bf16[128,24,384]{2,1,0:T(8,128)(2,1)}), bf16[128,24,384]{2,1,0:T(8,128)(2,1)S(1)}, u32[]{:S(2)}, u32[]{:S(2)}) async-start(bf16[128,24,384]{2,1,0:T(8,128)(2,1)} %get-tuple-element.10), calls=%async_computation | async-start | bytes 4718592 | tf_op jit(solution)/shard_map/all_to_all | solution.py:529
  174.5 0.0 copy-start
  174.5 1.7 copy-done
  176.1 3.6 %shard_map.88 = (bf16[1536,768]{1,0:T(8,128)(2,1)S(1)}, bf16[1536,768]{1,0:T(8,128)(2,1)S(1)}, bf16[1536,768]{1,0:T(8,128)(2,1)S(1)}) custom-call(bf16[128,24,384]{2,1,0:T(8,128)(2,1)S(1)} %copy-done), custom_call_target="tpu_custom_call" | custom-call | bytes 10485760 | tf_op jit(solution)/shard_map/pallas_call | solution.py:460
  179.8 0.0 copy-start.1
  179.8 1.4 copy-done.1
  181.2 0.0 copy-start.3
  181.2 1.4 copy-done.3
  182.5 6.5 %convolution_convert_fusion.2 = bf16[768,1280]{1,0:T(8,128)(2,1)} fusion(bf16[1536,768]{1,0:T(8,128)(2,1)S(1)} %get-tuple-element.12, bf16[1536,1280]{1,0:T(8,128)(2,1)} %bitcast.22), kind=kOutput, calls=%fused_computation.3 | convolution fusion | flops 3020881920 | bytes 8257536 | tf_op jit(solution)/shard_map/dot_general | solution.py:534
  189.1 0.2 broadcast_in_dim_reshape.8.spot_ref
  189.3 0.0 copy-start.2
  189.3 6.3 %convolution_convert_fusion.1 = bf16[768,1280]{1,0:T(8,128)(2,1)S(1)} fusion(bf16[1536,768]{1,0:T(8,128)(2,1)} %copy-done.3, bf16[1536,1280]{1,0:T(8,128)(2,1)} %bitcast.21), kind=kOutput, calls=%fused_computation.2 | convolution fusion | flops 3020881920 | bytes 8257536 | tf_op jit(solution)/shard_map/dot_general | solution.py:534
  195.6 0.0 copy-done.2
  195.6 0.0 copy-start.4
  195.6 6.6 %convolution_convert_fusion = bf16[768,1536]{1,0:T(8,128)(2,1)S(1)} fusion(bf16[1536,768]{1,0:T(8,128)(2,1)S(1)} %copy-done.2, bf16[1536,1536]{1,0:T(8,128)(2,1)} %bitcast.20), kind=kOutput, calls=%fused_computation.1 | convolution fusion | flops 3625058304 | bytes 9437184 | tf_op jit(solution)/shard_map/dot_general | solution.py:534
  202.2 0.0 copy-done.4
  202.2 3.2 %maximum_bitcast_fusion = bf16[1,768,4096]{2,1,0:T(8,128)(2,1)} fusion(bf16[768,1536]{1,0:T(8,128)(2,1)S(1)} %convolution_convert_fusion, bf16[768,1280]{1,0:T(8,128)(2,1)S(1)} %convolution_convert_fusion.1, bf16[768,1280]{1,0:T(8,128)(2,1)S(1)} %copy-done.4), kind=kLoop, calls=%fused_computation | loop fusion | flops 18874368 | bytes 12582912 | tf_op jit(solution)/shard_map/broadcast_in_dim | solution.py:544
  205.4 2.5 %all-to-all-done.got_ref = bf16[128,24,384]{2,1,0:T(8,128)(2,1)S(1)} async-done(((bf16[128,24,384]{2,1,0:T(8,128)(2,1)}), bf16[128,24,384]{2,1,0:T(8,128)(2,1)S(1)}, u32[]{:S(2)}, u32[]{:S(2)}) %all-to-all-start) | async-done | bytes 2359328 | tf_op jit(solution)/shard_map/all_to_all | solution.py:529
  207.9 4.5 %shard_map.87 = bf16[1024,768]{1,0:T(8,128)(2,1)} custom-call(s32[1024,1]{1,0:T(8,128)S(1)} %broadcast_in_dim_reshape.8.spot_ref, bf16[128,24,384]{2,1,0:T(8,128)(2,1)S(1)} %all-to-all-done.got_ref), custom_call_target="tpu_custom_call" | custom-call | tf_op jit(solution)/shard_map/pallas_call | solution.py:491
  (1 shorter events, 0.0 us)
Async XLA Ops:
  166.5 41.4 %all-to-all-start = ((bf16[128,24,384]{2,1,0:T(8,128)(2,1)}), bf16[128,24,384]{2,1,0:T(8,128)(2,1)S(1)}, u32[]{:S(2)}, u32[]{:S(2)}) async-start(bf16[128,24,384]{2,1,0:T(8,128)(2,1)} %get-tuple-element.10), calls=%async_computation | async-start | bytes 4718592 | tf_op jit(solution)/shard_map/all_to_all | solution.py:529
  174.5 1.7 copy-start
  179.8 1.4 copy-start.1
  181.2 1.4 copy-start.3
  189.3 6.3 %copy-start.2 = (bf16[1536,768]{1,0:T(8,128)(2,1)S(1)}, bf16[1536,768]{1,0:T(8,128)(2,1)}, u32[]{:S(2)}) copy-start(bf16[1536,768]{1,0:T(8,128)(2,1)} %copy-done.1) | copy-start | bytes 7077892
  195.6 6.6 %copy-start.4 = (bf16[768,1280]{1,0:T(8,128)(2,1)S(1)}, bf16[768,1280]{1,0:T(8,128)(2,1)}, u32[]{:S(2)}) copy-start(bf16[768,1280]{1,0:T(8,128)(2,1)} %convolution_convert_fusion.2) | copy-start | bytes 5898244

commit v7 on v6

--- a/solution.py
+++ b/solution.py
@@ -433,8 +433,14 @@
     )(*operands)
 
 
-def arrange_kernel(got_ref, *out_refs):
-    for part in range(3):
+TILE = 256
+
+
+def weight_grad_kernel(got_ref, scaled0, scaled1, scaled2, out_ref, rows, turned):
+    step = pl.program_id(0)
+    for part, scaled in enumerate((scaled0, scaled1, scaled2)):
+        first_step = STARTS[part] // TILE
+        last_step = first_step + WIDTHS[part] // TILE
 
         def block_of(block, carry, part=part):
             pieces = []
@@ -444,27 +450,46 @@
                 coords[(part + 1) % 3] = block % SIDE
                 coords[(part + 2) % 3] = block // 8
                 group, owner = place(coords, (block // SIDE) % 2)
-                rows = got_ref[group * 32 + owner].astype(jnp.float32)
-                pieces.append(jnp.concatenate([rows[:CAP], rows[CAP:]], axis=1))
+                piece = got_ref[group * 32 + owner].astype(jnp.float32)
+                pieces.append(jnp.concatenate([piece[:CAP], piece[CAP:]], axis=1))
             first = pl.multiple_of(block * PICK, PICK)
-            out_refs[part][pl.ds(first, PICK)] = jnp.concatenate(pieces, axis=0).astype(
-                jnp.bfloat16
-            )
+            rows[pl.ds(first, PICK)] = jnp.concatenate(pieces, axis=0)
             return carry
 
-        lax.fori_loop(0, 32, block_of, 0)
-
-
-def arrange(got):
-    vmem = pl.BlockSpec(memory_space=pltpu.VMEM)
+        @pl.when(step == first_step)
+        def _():
+            lax.fori_loop(0, 32, block_of, 0)
+            for first in range(0, 1536, 128):
+                turned[:, first : first + 128] = rows[first : first + 128].T.astype(jnp.bfloat16)
+
+        @pl.when((step >= first_step) & (step < last_step))
+        def _():
+            out_ref[...] = jnp.dot(
+                turned[...], scaled[...], preferred_element_type=jnp.float32
+            ).astype(jnp.bfloat16)
+
+
+def weight_gradient(got, parts):
+    def columns(part):
+        first, count = STARTS[part] // TILE, WIDTHS[part] // TILE
+        return pl.BlockSpec((1536, TILE), lambda i: (0, jnp.clip(i - first, 0, count - 1)))
+
     return pl.pallas_call(
-        arrange_kernel,
-        out_shape=[jax.ShapeDtypeStruct((1536, 768), jnp.bfloat16)] * 3,
-        in_specs=[vmem],
-        out_specs=[vmem] * 3,
-        compiler_params=pltpu.CompilerParams(vmem_limit_bytes=24 << 20),
-        cost_estimate=pl.CostEstimate(flops=0, bytes_accessed=10 << 20, transcendentals=0),
-    )(got)
+        weight_grad_kernel,
+        grid=(4096 // TILE,),
+        out_shape=jax.ShapeDtypeStruct((768, 4096), jnp.bfloat16),
+        in_specs=[pl.BlockSpec((128, 2 * CAP, 384), lambda i: (0, 0, 0))]
+        + [columns(part) for part in range(3)],
+        out_specs=pl.BlockSpec((768, TILE), lambda i: (0, i)),
+        scratch_shapes=[
+            pltpu.VMEM((1536, 768), jnp.float32),
+            pltpu.VMEM((768, 1536), jnp.bfloat16),
+        ],
+        compiler_params=pltpu.CompilerParams(vmem_limit_bytes=40 << 20),
+        cost_estimate=pl.CostEstimate(
+            flops=2 * 1536 * 768 * 4096, bytes_accessed=24 << 20, transcendentals=0
+        ),
+    )(got, *[rows.reshape(1536, width) for rows, width in zip(parts, WIDTHS)])
 
 
 def restore_kernel(spot_ref, got_ref, out_ref, rows):
@@ -530,16 +555,7 @@
 
     got_hidden = parts[4]
     returned = exchange(parts[3])
-    grads = [
-        lax.dot_general(
-            rows,
-            part.reshape(1536, width),
-            (((0,), (0,)), ((), ())),
-            preferred_element_type=jnp.float32,
-        ).astype(jnp.bfloat16)
-        for rows, part, width in zip(arrange(got_hidden), parts[:3], WIDTHS)
-    ]
-    weight_grad = jnp.concatenate(grads, axis=1)
+    weight_grad = weight_gradient(got_hidden, parts[:3])
     hidden_grad = restore(spot[:, None], returned)
     return hidden_grad.reshape(128, 8, 768), weight_grad[None]
 

time: 213 us -> 213 us (level)
  matrix products: 19.5 us -> 0.13 us
  Pallas kernels: 171 us -> 189 us
  other arithmetic: 4.52 us -> 1.33 us
  waiting for transfers between devices: 2.49 us -> 5.06 us
    dot_general x3 -> x0, matrix products: 19.4 us -> none  [shards(): lax.dot_general(rows, part.reshape(1536, width), (((0,), (0,)), ((), ()))...]
    pallas_call x1, Pallas kernels: 3.63 us -> 22.3 us  [weight_gradient(): pl.pallas_call(weight_grad_kernel, grid=(4096 // TILE,), out_shape=jax.Sh...]
    broadcast_in_dim x1 -> x0, other arithmetic: 3.2 us -> none  [shards(): return (hidden_grad.reshape(128, 8, 768), weight_grad[None])]
    all_to_all x1, waiting for transfers between devices: 2.49 us -> 5.06 us  [exchange(): lax.all_to_all(rows, ('grp', 'ep'), split_axis=0, concat_axis=0, tiled=True)]
    unnamed x11 -> x7, local copies, waits for them, and re-layouts: 5.24 us -> 6.67 us
  transfers between devices with their start and end apart: 1 -> 1, of which waited for: 1 -> 1; matrix products, arithmetic and copies ran while one was open for 11% -> 0% of each run, Pallas kernels for 2% -> 10%
where the time goes in v7:
time: 213 us; the launch traced here: 212 us
  Pallas kernels  189 us (89%)
  starting transfers between devices  7.99 us (4%)
  local copies, waits for them, and re-layouts  7.7 us (4%)
  waiting for transfers between devices  5.06 us (2%)
    pallas_call x1, Pallas kernels, dispatch(): pl.pallas_call(dispatch_kernel, out_shape=shapes, in_specs=[vmem] * 7 + [...  163 us
    pallas_call x1, Pallas kernels, weight_gradient(): pl.pallas_call(weight_grad_kernel, grid=(4096 // TILE,), out_shape=jax.Sh...  22.3 us
    all_to_all x1, starting transfers between devices, exchange(): lax.all_to_all(rows, ('grp', 'ep'), split_axis=0, concat_axis=0, tiled=True)  7.99 us
    unnamed x7, local copies, waits for them, and re-layouts  6.67 us
    all_to_all x1, waiting for transfers between devices, exchange(): lax.all_to_all(rows, ('grp', 'ep'), split_axis=0, concat_axis=0, tiled=True)  5.06 us
    pallas_call x1, Pallas kernels, restore(): pl.pallas_call(restore_kernel, out_shape=jax.ShapeDtypeStruct((1024, 768)...  4.46 us
  transfers between devices with their start and end apart: 1, of which 1 were waited for; matrix products, arithmetic and copies ran while one was open for 0% of the time, Pallas kernels for 10%

profile of v7, /device:TPU:1, one launch (start us, length us, event | category | flops | bytes accessed | tf_op | source)
XLA Modules:
  0.0 212.3 jit_solution(16342870090243314358)
XLA Ops:
  0.6 0.8 copy.20
  1.4 0.2 fusion.1
  1.7 0.1 fusion.2
  1.8 0.4 select_reduce_fusion
  2.2 0.7 convert_add_fusion
  2.9 0.1 copy.22
  3.0 0.7 broadcast_in_dim_reshape.7.spot_ref
  3.7 162.7 %shard_map.86 = (bf16[8,4,48,1280]{3,2,1,0:T(8,128)(2,1)}, bf16[8,4,48,1280]{3,2,1,0:T(8,128)(2,1)}, bf16[8,4,48,1536]{3,2,1,0:T(8,128)(2,1)}, bf16[128,24,384]{2,1,0:T(8,128)(2,1)}, bf16[128,24,384]{2,1,0:T(8,128)(2,1)}) custom-call(s32[8,128]{1,0:T(8,128)} %bitcast.13, f32[8,128]{1,0:T(8,128)} %bitcast.14, s32[1,128]{1,0:T(1,128)} %rollout_ref.1, ...), custom_call_target="tpu_custom_call" | custom-call | tf_op jit(solution)/shard_map/pallas_call | solution.py:424
  166.5 8.0 %all-to-all-start = ((bf16[128,24,384]{2,1,0:T(8,128)(2,1)}), bf16[128,24,384]{2,1,0:T(8,128)(2,1)S(1)}, u32[]{:S(2)}, u32[]{:S(2)}) async-start(bf16[128,24,384]{2,1,0:T(8,128)(2,1)} %get-tuple-element.7), calls=%async_computation | async-start | bytes 4718592 | tf_op jit(solution)/shard_map/all_to_all | solution.py:554
  174.5 0.2 broadcast_in_dim_reshape.8.spot_ref
  174.6 0.0 copy-start
  174.7 2.1 copy-done
  176.8 0.0 copy-start.1
  176.8 2.1 copy-done.1
  178.9 0.0 copy-start.2
  178.9 1.7 copy-done.2
  180.5 22.3 %shard_map.88 = bf16[768,4096]{1,0:T(8,128)(2,1)} custom-call(bf16[128,24,384]{2,1,0:T(8,128)(2,1)S(1)} %copy-done.2, bf16[1536,1280]{1,0:T(8,128)(2,1)S(1)} %bitcast.9, bf16[1536,1280]{1,0:T(8,128)(2,1)S(1)} %bitcast.10, bf16[1536,1536]{1,0:T(8,128)(2,1)} %bitcast.15), custom_call_target="tpu_custom_call" | custom-call | flops 9663676416 | bytes 25165824 | tf_op jit(solution)/shard_map/pallas_call | solution.py:477
  202.8 5.1 %all-to-all-done.got_ref = bf16[128,24,384]{2,1,0:T(8,128)(2,1)S(1)} async-done(((bf16[128,24,384]{2,1,0:T(8,128)(2,1)}), bf16[128,24,384]{2,1,0:T(8,128)(2,1)S(1)}, u32[]{:S(2)}, u32[]{:S(2)}) %all-to-all-start) | async-done | bytes 2359328 | tf_op jit(solution)/shard_map/all_to_all | solution.py:554
  207.9 4.5 %shard_map.87 = bf16[1024,768]{1,0:T(8,128)(2,1)} custom-call(s32[1024,1]{1,0:T(8,128)S(1)} %broadcast_in_dim_reshape.8.spot_ref, bf16[128,24,384]{2,1,0:T(8,128)(2,1)S(1)} %all-to-all-done.got_ref), custom_call_target="tpu_custom_call" | custom-call | tf_op jit(solution)/shard_map/pallas_call | solution.py:516
  (1 shorter events, 0.0 us)
Async XLA Ops:
  166.5 41.4 %all-to-all-start = ((bf16[128,24,384]{2,1,0:T(8,128)(2,1)}), bf16[128,24,384]{2,1,0:T(8,128)(2,1)S(1)}, u32[]{:S(2)}, u32[]{:S(2)}) async-start(bf16[128,24,384]{2,1,0:T(8,128)(2,1)} %get-tuple-element.7), calls=%async_computation | async-start | bytes 4718592 | tf_op jit(solution)/shard_map/all_to_all | solution.py:554
  174.6 2.1 copy-start
  176.8 2.1 copy-start.1
  178.9 1.7 copy-start.2

commit v8 on v7

--- a/solution.py
+++ b/solution.py
@@ -344,22 +344,20 @@
         return carry
 
     def onward(step, carry):
-        @pl.when(step < SIDE)
-        def _():
-            turn = jnp.where(step < 3, 2 * step - 1, 2)
-            for part in range(3):
-                mid_copy(part, turn).wait()
-            forward(turn, [mids[part].at[turn - 1] for part in range(3)])
-
-        @pl.when(step < SIDE)
-        def _():
-            lax.fori_loop(43 * step - 42, jnp.minimum(43 * step + 1, 128), push, 0)
-
+        turn = jnp.where(step < 3, 2 * step - 1, 2)
+        for part in range(3):
+            mid_copy(part, turn).wait()
+        forward(turn, [mids[part].at[turn - 1] for part in range(3)])
+        lax.fori_loop(43 * step - 42, jnp.minimum(43 * step + 1, 128), push, 0)
+        return carry
+
+    def gain(step, carry):
         for part in range(3):
             absorb(part, jnp.where(step < 2, 0, jnp.where(step < 4, 2 * step - 3, 2)))
         return carry
 
-    lax.fori_loop(1, SIDE + 1, onward, 0)
+    lax.fori_loop(1, SIDE, onward, 0)
+    lax.fori_loop(1, SIDE + 1, gain, 0)
 
     def settle(index, carry):
         hidden_copy(index).wait_send()

time: 213 us -> 213 us (level)
  no operation moved by 1% of the time
where the time goes in v8:
time: 213 us; the launch traced here: 212 us
  Pallas kernels  189 us (89%)
  starting transfers between devices  7.99 us (4%)
  local copies, waits for them, and re-layouts  7.7 us (4%)
  waiting for transfers between devices  5.06 us (2%)
    pallas_call x1, Pallas kernels, dispatch(): pl.pallas_call(dispatch_kernel, out_shape=shapes, in_specs=[vmem] * 7 + [...  163 us
    pallas_call x1, Pallas kernels, weight_gradient(): pl.pallas_call(weight_grad_kernel, grid=(4096 // TILE,), out_shape=jax.Sh...  22.3 us
    all_to_all x1, starting transfers between devices, exchange(): lax.all_to_all(rows, ('grp', 'ep'), split_axis=0, concat_axis=0, tiled=True)  7.99 us
    unnamed x7, local copies, waits for them, and re-layouts  6.67 us
    all_to_all x1, waiting for transfers between devices, exchange(): lax.all_to_all(rows, ('grp', 'ep'), split_axis=0, concat_axis=0, tiled=True)  5.06 us
    pallas_call x1, Pallas kernels, restore(): pl.pallas_call(restore_kernel, out_shape=jax.ShapeDtypeStruct((1024, 768)...  4.46 us
  transfers between devices with their start and end apart: 1, of which 1 were waited for; matrix products, arithmetic and copies ran while one was open for 0% of the time, Pallas kernels for 10%

profile of v8, /device:TPU:1, one launch (start us, length us, event | category | flops | bytes accessed | tf_op | source)
XLA Modules:
  0.0 212.3 jit_solution(12854344212850816874)
XLA Ops:
  0.6 0.8 copy.20
  1.4 0.2 fusion.1
  1.7 0.1 fusion.2
  1.8 0.4 select_reduce_fusion
  2.2 0.7 convert_add_fusion
  2.9 0.1 copy.22
  3.0 0.7 broadcast_in_dim_reshape.7.spot_ref
  3.7 162.7 %shard_map.86 = (bf16[8,4,48,1280]{3,2,1,0:T(8,128)(2,1)}, bf16[8,4,48,1280]{3,2,1,0:T(8,128)(2,1)}, bf16[8,4,48,1536]{3,2,1,0:T(8,128)(2,1)}, bf16[128,24,384]{2,1,0:T(8,128)(2,1)}, bf16[128,24,384]{2,1,0:T(8,128)(2,1)}) custom-call(s32[8,128]{1,0:T(8,128)} %bitcast.13, f32[8,128]{1,0:T(8,128)} %bitcast.14, s32[1,128]{1,0:T(1,128)} %rollout_ref.1, ...), custom_call_target="tpu_custom_call" | custom-call | tf_op jit(solution)/shard_map/pallas_call | solution.py:422
  166.5 8.0 %all-to-all-start = ((bf16[128,24,384]{2,1,0:T(8,128)(2,1)}), bf16[128,24,384]{2,1,0:T(8,128)(2,1)S(1)}, u32[]{:S(2)}, u32[]{:S(2)}) async-start(bf16[128,24,384]{2,1,0:T(8,128)(2,1)} %get-tuple-element.7), calls=%async_computation | async-start | bytes 4718592 | tf_op jit(solution)/shard_map/all_to_all | solution.py:552
  174.5 0.2 broadcast_in_dim_reshape.8.spot_ref
  174.6 0.0 copy-start
  174.7 2.1 copy-done
  176.8 0.0 copy-start.1
  176.8 2.1 copy-done.1
  178.9 0.0 copy-start.2
  178.9 1.7 copy-done.2
  180.5 22.3 %shard_map.88 = bf16[768,4096]{1,0:T(8,128)(2,1)} custom-call(bf16[128,24,384]{2,1,0:T(8,128)(2,1)S(1)} %copy-done.2, bf16[1536,1280]{1,0:T(8,128)(2,1)S(1)} %bitcast.9, bf16[1536,1280]{1,0:T(8,128)(2,1)S(1)} %bitcast.10, bf16[1536,1536]{1,0:T(8,128)(2,1)} %bitcast.15), custom_call_target="tpu_custom_call" | custom-call | flops 9663676416 | bytes 25165824 | tf_op jit(solution)/shard_map/pallas_call | solution.py:475
  202.8 5.1 %all-to-all-done.got_ref = bf16[128,24,384]{2,1,0:T(8,128)(2,1)S(1)} async-done(((bf16[128,24,384]{2,1,0:T(8,128)(2,1)}), bf16[128,24,384]{2,1,0:T(8,128)(2,1)S(1)}, u32[]{:S(2)}, u32[]{:S(2)}) %all-to-all-start) | async-done | bytes 2359328 | tf_op jit(solution)/shard_map/all_to_all | solution.py:552
  207.9 4.5 %shard_map.87 = bf16[1024,768]{1,0:T(8,128)(2,1)} custom-call(s32[1024,1]{1,0:T(8,128)S(1)} %broadcast_in_dim_reshape.8.spot_ref, bf16[128,24,384]{2,1,0:T(8,128)(2,1)S(1)} %all-to-all-done.got_ref), custom_call_target="tpu_custom_call" | custom-call | tf_op jit(solution)/shard_map/pallas_call | solution.py:514
  (1 shorter events, 0.0 us)
Async XLA Ops:
  166.5 41.4 %all-to-all-start = ((bf16[128,24,384]{2,1,0:T(8,128)(2,1)}), bf16[128,24,384]{2,1,0:T(8,128)(2,1)S(1)}, u32[]{:S(2)}, u32[]{:S(2)}) async-start(bf16[128,24,384]{2,1,0:T(8,128)(2,1)} %get-tuple-element.7), calls=%async_computation | async-start | bytes 4718592 | tf_op jit(solution)/shard_map/all_to_all | solution.py:552
  174.6 2.1 copy-start
  176.8 2.1 copy-start.1
  178.9 1.7 copy-start.2
